TPU v7x, 32 devices: a whole 2x2x4 slice. The times are simulated.
32 devices in a mesh: dp: 4 (over y, x), ctx: 2 (over core), tp: 4 (over z).
Axes of the slice: x: 2, y: 2, z: 4, core: 2. Of those that a mesh axis runs over, the one named last changes fastest.
Arguments:
- query_branch: bfloat16 [2048, 8192], P(('dp', 'ctx'), 'tp'), parts along dimension 0, may hold values from -6 to 6
- key_branch: bfloat16 [2048, 8192], P(('dp', 'ctx'), 'tp'), parts along dimension 0, may hold values from -6 to 6
- value_branch: bfloat16 [2048, 8192], P(('dp', 'ctx'), 'tp'), parts along dimension 0, may hold values from -6 to 6
- output_grad: bfloat16 [2048, 8192], P(('dp', 'ctx'), 'tp'), parts along dimension 0, may hold values from -6 to 6
- residues: float32 [8192, 8], P('tp'), may hold values from -4 to 4
- decay_rates: float32 [8192, 8], P('tp'), as said below
Outputs:
- mixed_out: bfloat16 [2048, 8192], P(('dp', 'ctx'), 'tp'), parts along dimension 0
- query_grad: bfloat16 [2048, 8192], P(('dp', 'ctx'), 'tp'), parts along dimension 0
- key_grad: bfloat16 [2048, 8192], P(('dp', 'ctx'), 'tp'), parts along dimension 0
- value_grad: bfloat16 [2048, 8192], P(('dp', 'ctx'), 'tp'), parts along dimension 0
- residue_grad: float32 [32768, 8], P(('dp', 'tp')), parts along dimension 0
There are 4 independent parts, one for each index of `dp`. A program takes and returns all parts, laid end to end along the dimension named above; an argument that names none is the same for every part. Nothing has to cross between parts.
Inputs may be any that keep to these rules, and one draw needn't show every extreme that they name: `decay_rates`: every rate lies between 0.5 / 512 and 100 / 512.
All inputs are finite; a program needn't handle non-finite values.
Results may differ from a plain program's by a relative error of at most 0.01.
Values may be sent and summed in bfloat16 or wider, within the bound.
No kernel may reach another device: no remote copies, remote signals or barrier semaphores. Data moves between devices by JAX's collectives and lax.ppermute only.
A program may use at most 128 MiB of HBM per device.

v0:
```python
import functools

import jax
import jax.numpy as jnp
from jax import lax
from jax.experimental import pallas as pl
from jax.experimental.pallas import tpu as pltpu
from jax.sharding import PartitionSpec as P

F32 = jnp.float32
BF16 = jnp.bfloat16
LANES = 128
GROUPS = 8
BLOCK = GROUPS * LANES
PAD = 8
UNROLL = 8


def one_minus_exp_2(rate, factor):
    square = rate * rate
    sinh = rate * (1.0 + square * (1 / 6 + square * (1 / 120 + square * (1 / 5040))))
    return 2.0 * factor * sinh


def mode_tables(rates, residues, table):
    modes, channels = rates.shape
    factor = jnp.exp(-rates)
    scale = jnp.sqrt(one_minus_exp_2(rates, factor) / modes)
    weight = residues * scale
    groups = channels // LANES
    for group in range(groups):
        lanes = slice(group * LANES, (group + 1) * LANES)
        table[pl.ds(group * modes, modes), :] = factor[:, lanes]
        table[pl.ds((groups + group) * modes, modes), :] = weight[:, lanes]
    return scale


def table_rows(table, which, half, modes, groups):
    start = (which * groups + half * GROUPS) * modes
    return [table[pl.ds(start + mode, GROUPS, stride=modes), :] for mode in range(modes)]


def tree_sum(terms):
    while len(terms) > 1:
        terms = [
            terms[i] + terms[i + 1] if i + 1 < len(terms) else terms[i]
            for i in range(0, len(terms), 2)
        ]
    return terms[0]


class Shape:
    def __init__(self, length, channels, modes):
        self.length = length
        self.channels = channels
        self.modes = modes
        self.halves = channels // BLOCK
        self.groups = channels // LANES
        self.chunk = min(64, length)
        self.chunks = length // self.chunk
        self.stride = length + PAD
        self.rows = self.halves * GROUPS * self.stride


def lanes_of(half):
    return slice(half * BLOCK, (half + 1) * BLOCK)


def products(shape, half, token, inputs, wide):
    step = min(32, shape.chunk)

    def body(i, carry):
        at = pl.multiple_of(token + i * step, step)
        for group in range(GROUPS):
            lane = slice(half * BLOCK + group * LANES, half * BLOCK + (group + 1) * LANES)
            row = pl.multiple_of((half * GROUPS + group) * shape.stride + at, 8)
            q, dy, v, k = [inputs[j, pl.ds(at, step), lane] for j in range(4)]
            wide[0, pl.ds(row, step), :] = (k * v).astype(F32)
            wide[1, pl.ds(row, step), :] = (dy * q).astype(F32)
        return carry

    lax.fori_loop(0, shape.chunk // step, body, 0)


def recurrence(shape, half, direction, chunk_index, factor, weight, state, dot, wide, conv):
    sign = 1 - 2 * direction
    begin = direction * (shape.length - 1) + sign * chunk_index * shape.chunk
    base = half * GROUPS * shape.stride
    modes = shape.modes

    def body(i, carry):
        state, dot = list(carry[0]), list(carry[1])
        for j in range(UNROLL):
            row = base + begin + sign * (i * UNROLL + j)
            rows = pl.ds(row, GROUPS, stride=shape.stride)
            source = wide[direction, rows, :]
            other = wide[1 - direction, rows, :] if dot else None
            terms = []
            for mode in range(modes):
                state[mode] = factor[mode] * state[mode] + source
                if weight is not None:
                    terms.append(weight[mode] * state[mode])
                if dot:
                    dot[mode] = dot[mode] + other * state[mode]
            if weight is not None:
                conv[rows, :] = tree_sum(terms)
        return tuple(state), tuple(dot)

    state, dot = lax.fori_loop(0, shape.chunk // UNROLL, body, (tuple(state), tuple(dot)))
    return list(state), list(dot)


def outputs(shape, half, token, pair, inputs, conv, staged):
    step = min(32, shape.chunk)

    def body(i, carry):
        at = pl.multiple_of(token + i * step, step)
        for group in range(GROUPS):
            lane = slice(half * BLOCK + group * LANES, half * BLOCK + (group + 1) * LANES)
            row = pl.multiple_of((half * GROUPS + group) * shape.stride + at, 8)
            value = conv[pl.ds(row, step), :]
            for j in range(2):
                staged[j, pl.ds(at, step), lane] = (
                    inputs[2 * pair + j, pl.ds(at, step), lane].astype(F32) * value
                ).astype(BF16)
        return carry

    lax.fori_loop(0, shape.chunk // step, body, 0)


def token_of(shape, direction, chunk_index):
    last = shape.chunks - 1
    return pl.multiple_of(
        (chunk_index + direction * (last - 2 * chunk_index)) * shape.chunk, shape.chunk
    )


def in_copy(shape, j, half, direction, chunk, source, inputs, sem):
    where = (pl.ds(token_of(shape, direction, chunk), shape.chunk), lanes_of(half))
    return pltpu.make_async_copy(
        source.at[where], inputs.at[(j,) + where], sem.at[j, half * shape.chunks + chunk]
    )


def out_copy(shape, j, half, direction, chunk, staged, target, sem):
    where = (pl.ds(token_of(shape, direction, chunk), shape.chunk), lanes_of(half))
    return pltpu.make_async_copy(
        staged.at[(j,) + where], target.at[where], sem.at[j, half * shape.chunks + chunk]
    )


def send_out(shape, half, pair, direction, chunk, staged, targets, sem):
    for p in range(2):

        @pl.when(pair == p)
        def _():
            for j in range(2):
                out_copy(shape, j, half, direction, chunk, staged, targets[2 * p + j], sem).start()


def wait_out(shape, direction, staged, targets, sem):
    for half in range(shape.halves):
        for chunk in range(shape.chunks):
            for j in range(2):
                out_copy(shape, j, half, direction, chunk, staged, targets[j], sem).wait()


def first_kernel(
    shape, q, dy, v, k, rates_hbm, res_hbm,
    out0, out1, out2, out3, wide, inputs, sent, table, scale,
    conv, staged, rates, res, in_sem, coef_sem, out_sem,
):
    direction = lax.axis_index("ctx")
    sources = (q, dy, v, k)
    targets = (out0, out1, out2, out3)
    coef = [
        pltpu.make_async_copy(rates_hbm, rates, coef_sem.at[0]),
        pltpu.make_async_copy(res_hbm, res, coef_sem.at[1]),
    ]
    for copy in coef:
        copy.start()
    for half in range(shape.halves):
        for chunk in range(shape.chunks):
            for j in range(4):
                in_copy(shape, j, half, direction, chunk, sources[j], inputs, in_sem).start()
    for copy in coef:
        copy.wait()
    scale[...] = mode_tables(rates[...], res[...], table)
    zero = jnp.zeros((GROUPS, LANES), F32)
    for half in range(shape.halves):
        factor = table_rows(table, 0, half, shape.modes, shape.groups)
        weight = table_rows(table, 1, half, shape.modes, shape.groups)

        def body(chunk, carry):
            token = token_of(shape, direction, chunk)
            for j in range(4):
                in_copy(shape, j, half, direction, chunk, sources[j], inputs, in_sem).wait()
            products(shape, half, token, inputs, wide)
            state, dot = recurrence(
                shape, half, direction, chunk, factor, weight, carry[0], carry[1], wide, conv
            )
            outputs(shape, half, token, direction, inputs, conv, staged)
            send_out(shape, half, direction, direction, chunk, staged, targets, out_sem)
            return tuple(state), tuple(dot)

        zeros = (zero,) * shape.modes
        state, dot = lax.fori_loop(0, shape.chunks, body, (zeros, zeros))
        rows = slice(half * GROUPS, (half + 1) * GROUPS)
        for mode in range(shape.modes):
            sent[0, mode, rows, :] = state[mode].astype(BF16)
            sent[1, mode, rows, :] = dot[mode].astype(BF16)
    wait_out(shape, direction, staged, targets, out_sem)


def second_kernel(
    shape, in0, in1, in2, in3, wide, inputs, sent, table, scale, received,
    out0, out1, out2, out3, residue,
    conv, staged, totals, out_sem,
):
    del in0, in1, in2, in3
    direction = 1 - lax.axis_index("ctx")
    targets = (out0, out1, out2, out3)
    modes = shape.modes
    for half in range(shape.halves):
        rows = slice(half * GROUPS, (half + 1) * GROUPS)
        factor = table_rows(table, 0, half, modes, shape.groups)
        weight = table_rows(table, 1, half, modes, shape.groups)
        state = []
        for mode in range(modes):
            mine = sent[0, mode, rows, :].astype(F32)
            theirs = received[0, mode, rows, :].astype(F32)
            dots = sent[1, mode, rows, :].astype(F32) + received[1, mode, rows, :].astype(F32)
            totals[pl.ds((half * modes + mode) * GROUPS, GROUPS), :] = (
                dots + factor[mode] * (mine * theirs)
            )
            state.append(theirs)
        for group in range(GROUPS):
            lane = slice(half * BLOCK + group * LANES, half * BLOCK + (group + 1) * LANES)
            picked = totals[pl.ds(half * modes * GROUPS + group, modes, stride=GROUPS), :]
            residue[:, lane] = picked * scale[:, lane]

        def body(chunk, state):
            token = token_of(shape, direction, chunk)
            state, _ = recurrence(
                shape, half, direction, chunk, factor, weight, state, (), wide, conv
            )
            outputs(shape, half, token, direction, inputs, conv, staged)
            send_out(shape, half, direction, direction, chunk, staged, targets, out_sem)
            return tuple(state)

        lax.fori_loop(0, shape.chunks, body, tuple(state))
    wait_out(shape, direction, staged, targets, out_sem)


def ends_kernel(
    shape, q, dy, v, k, rates_hbm, res_hbm,
    wide, inputs, ends, table, scale,
    rates, res, in_sem, coef_sem,
):
    sources = (q, dy, v, k)
    coef = [
        pltpu.make_async_copy(rates_hbm, rates, coef_sem.at[0]),
        pltpu.make_async_copy(res_hbm, res, coef_sem.at[1]),
    ]
    for copy in coef:
        copy.start()
    for half in range(shape.halves):
        for chunk in range(shape.chunks):
            for j in range(4):
                in_copy(shape, j, half, 0, chunk, sources[j], inputs, in_sem).start()
    for copy in coef:
        copy.wait()
    scale[...] = mode_tables(rates[...], res[...], table)
    zeros = (jnp.zeros((GROUPS, LANES), F32),) * shape.modes
    for half in range(shape.halves):
        factor = table_rows(table, 0, half, shape.modes, shape.groups)

        def forward(chunk, carry):
            for j in range(4):
                in_copy(shape, j, half, 0, chunk, sources[j], inputs, in_sem).wait()
            products(shape, half, token_of(shape, 0, chunk), inputs, wide)
            state, dot = recurrence(
                shape, half, 0, chunk, factor, None, carry[0], carry[1], wide, None
            )
            return tuple(state), tuple(dot)

        def backward(chunk, state):
            state, _ = recurrence(shape, half, 1, chunk, factor, None, state, (), wide, None)
            return tuple(state)

        state, dot = lax.fori_loop(0, shape.chunks, forward, (zeros, zeros))
        back = lax.fori_loop(0, shape.chunks, backward, zeros)
        rows = slice(half * GROUPS, (half + 1) * GROUPS)
        for mode in range(shape.modes):
            ends[0, mode, rows, :] = state[mode]
            ends[1, mode, rows, :] = back[mode]
            ends[2, mode, rows, :] = dot[mode]


def both_kernel(
    shape, wide, inputs, starts, table,
    out0, out1, out2, out3,
    conv, staged, out_sem,
):
    targets = (out0, out1, out2, out3)
    for direction in range(2):
        for half in range(shape.halves):
            rows = slice(half * GROUPS, (half + 1) * GROUPS)
            factor = table_rows(table, 0, half, shape.modes, shape.groups)
            weight = table_rows(table, 1, half, shape.modes, shape.groups)
            state = tuple(starts[direction, mode, rows, :] for mode in range(shape.modes))

            def body(chunk, state):
                token = token_of(shape, direction, chunk)
                state, _ = recurrence(
                    shape, half, direction, chunk, factor, weight, state, (), wide, conv
                )
                outputs(shape, half, token, direction, inputs, conv, staged)
                for j in range(2):
                    out_copy(
                        shape, j, half, direction, chunk, staged, targets[2 * direction + j], out_sem
                    ).start()
                return tuple(state)

            lax.fori_loop(0, shape.chunks, body, state)
        wait_out(shape, direction, staged, targets[2 * direction :], out_sem)


HBM = pl.BlockSpec(memory_space=pltpu.HBM)
VMEM = pl.BlockSpec(memory_space=pltpu.VMEM)
LIMIT = 24 << 20


def pair(shape, arrays):
    modes, channels = shape.modes, shape.channels
    big = jax.ShapeDtypeStruct((shape.length, channels), BF16)
    copies = shape.halves * shape.chunks
    *outs, wide, inputs, sent, table, scale = pl.pallas_call(
        functools.partial(first_kernel, shape),
        in_specs=[HBM] * 6,
        out_specs=[HBM] * 4 + [VMEM] * 5,
        out_shape=[big] * 4
        + [
            pltpu.VMEM((2, shape.rows, LANES), F32),
            pltpu.VMEM((4, shape.length, channels), BF16),
            jax.ShapeDtypeStruct((2, modes, shape.groups, LANES), BF16),
            pltpu.VMEM((2 * modes * shape.groups, LANES), F32),
            pltpu.VMEM((modes, channels), F32),
        ],
        scratch_shapes=[
            pltpu.VMEM((shape.rows, LANES), F32),
            pltpu.VMEM((2, shape.length, channels), BF16),
            pltpu.VMEM((modes, channels), F32),
            pltpu.VMEM((modes, channels), F32),
            pltpu.SemaphoreType.DMA((4, copies)),
            pltpu.SemaphoreType.DMA((2,)),
            pltpu.SemaphoreType.DMA((2, copies)),
        ],
        compiler_params=pltpu.CompilerParams(vmem_limit_bytes=LIMIT),
        name="first",
    )(*arrays)
    received = lax.ppermute(sent, "ctx", [(0, 1), (1, 0)])
    *outs, residue = pl.pallas_call(
        functools.partial(second_kernel, shape),
        in_specs=[HBM] * 4 + [VMEM] * 6,
        out_specs=[HBM] * 4 + [VMEM],
        out_shape=[big] * 4 + [jax.ShapeDtypeStruct((modes, channels), F32)],
        input_output_aliases={0: 0, 1: 1, 2: 2, 3: 3},
        scratch_shapes=[
            pltpu.VMEM((shape.rows, LANES), F32),
            pltpu.VMEM((2, shape.length, channels), BF16),
            pltpu.VMEM((modes * shape.groups, LANES), F32),
            pltpu.SemaphoreType.DMA((2, copies)),
        ],
        compiler_params=pltpu.CompilerParams(vmem_limit_bytes=LIMIT),
        name="second",
    )(*outs, wide, inputs, sent, table, scale, received)
    return outs, residue


def many(shape, arrays, rates, owners):
    modes, channels = shape.modes, shape.channels
    big = jax.ShapeDtypeStruct((shape.length, channels), BF16)
    copies = shape.halves * shape.chunks
    wide, inputs, ends, table, scale = pl.pallas_call(
        functools.partial(ends_kernel, shape),
        in_specs=[HBM] * 6,
        out_specs=[VMEM] * 5,
        out_shape=[
            pltpu.VMEM((2, shape.rows, LANES), F32),
            pltpu.VMEM((4, shape.length, channels), BF16),
            jax.ShapeDtypeStruct((3, modes, shape.groups, LANES), F32),
            pltpu.VMEM((2 * modes * shape.groups, LANES), F32),
            jax.ShapeDtypeStruct((modes, channels), F32),
        ],
        scratch_shapes=[
            pltpu.VMEM((modes, channels), F32),
            pltpu.VMEM((modes, channels), F32),
            pltpu.SemaphoreType.DMA((4, copies)),
            pltpu.SemaphoreType.DMA((2,)),
        ],
        compiler_params=pltpu.CompilerParams(vmem_limit_bytes=LIMIT),
        name="ends",
    )(*arrays)
    rates = rates.reshape(modes, shape.groups, LANES)
    here = lax.axis_index("ctx")
    parts = lax.all_gather(ends[:2].astype(BF16), "ctx", axis=0).astype(F32)
    owner = jnp.arange(owners, dtype=jnp.int32)
    gaps = jnp.stack([here - 1 - owner, owner - 1 - here], axis=1).astype(F32)[:, :, None, None, None]
    decay = jnp.exp(-rates * shape.length * jnp.maximum(gaps, 0.0))
    starts = jnp.sum(jnp.where(gaps >= 0, decay, 0.0) * parts, axis=0)
    dots = ends[2] + jnp.exp(-rates) * ends[1] * starts[0]
    total = jnp.sum(lax.all_gather(dots.astype(BF16), "ctx", axis=0).astype(F32), axis=0)
    residue = total.reshape(modes, channels) * scale
    outs = pl.pallas_call(
        functools.partial(both_kernel, shape),
        in_specs=[VMEM] * 4,
        out_specs=[HBM] * 4,
        out_shape=[big] * 4,
        scratch_shapes=[
            pltpu.VMEM((shape.rows, LANES), F32),
            pltpu.VMEM((2, shape.length, channels), BF16),
            pltpu.SemaphoreType.DMA((2, copies)),
        ],
        compiler_params=pltpu.CompilerParams(vmem_limit_bytes=LIMIT),
        name="both",
    )(wide, inputs, starts, table)
    return outs, residue


def body(owners, query_branch, key_branch, value_branch, output_grad, residues, decay_rates):
    length, channels = query_branch.shape
    rates = decay_rates.T
    shape = Shape(length, channels, rates.shape[0])
    hbm = functools.partial(pltpu.with_memory_space_constraint, memory_space=pltpu.HBM)
    arrays = [
        hbm(array)
        for array in (query_branch, output_grad, value_branch, key_branch, rates, residues.T)
    ]
    outs, residue = pair(shape, arrays) if owners == 2 else many(shape, arrays, rates, owners)
    mixed_out, query_grad, key_grad, value_grad = outs
    return (mixed_out, query_grad, key_grad, value_grad, residue.T)


def solution(mesh):
    tokens = P(("dp", "ctx"), "tp")
    return jax.shard_map(
        functools.partial(body, mesh.shape["ctx"]),
        mesh=mesh,
        in_specs=(tokens,) * 4 + (P("tp", None),) * 2,
        out_specs=(tokens,) * 4 + (P(("dp", "tp"), None),),
        check_vma=False,
    )
```

profile of v0, /device:TPU:3, one launch (start us, length us, event | category | flops | bytes accessed | tf_op | source)
XLA Modules:
  0.0 15.3 jit_solution(9417117632162799490)
XLA Ops:
  0.6 7.8 %first.1 = (bf16[256,2048]{1,0:T(8,128)(2,1)}, bf16[256,2048]{1,0:T(8,128)(2,1)}, bf16[256,2048]{1,0:T(8,128)(2,1)}, bf16[256,2048]{1,0:T(8,128)(2,1)}, f32[2,42...) custom-call(bf16[256,2048]{1,0:T(8,128)(2,1)} %q.1, ...), custom_call_target="tpu_custom_call" | custom-call | tf_op jit(solution)/shard_map/first/pallas_call | solution.py:338
  8.5 0.7 %collective-permute-start = (bf16[2,8,16,128]{3,2,1,0:T(8,128)(2,1)S(1)}, bf16[2,8,16,128]{3,2,1,0:T(8,128)(2,1)S(1)}, u32[]{:S(2)}, u32[]{:S(2)}) collective-permute-start(bf16[2,8,16,128]{3,2,1,0:T(8,128)(2,1)S(1)} %get-tuple-element.25.sent), channel_id=1, source_target_pairs={{0,4},{4,0},{1,5},{5,1},{2,6},{6,2},{3,7},{7,3},{8,12},{12,8},{9,1... | collective-permute-start | bytes 196616 | tf_op jit(solution)/shard_map/ppermute | solution.py:362
  9.2 0.9 %collective-permute-done.received = bf16[2,8,16,128]{3,2,1,0:T(8,128)(2,1)S(1)} collective-permute-done((bf16[2,8,16,128]{3,2,1,0:T(8,128)(2,1)S(1)}, bf16[2,8,16,128]{3,2,1,0:T(8,128)(2,1)S(1)}, u32[]{:S(2)}, u32[]{:S(2)}) %collective-permute-start) | collective-permute-done | bytes 65568 | tf_op jit(solution)/shard_map/ppermute | solution.py:362
  10.1 5.2 %second.1 = (bf16[256,2048]{1,0:T(8,128)(2,1)}, bf16[256,2048]{1,0:T(8,128)(2,1)}, bf16[256,2048]{1,0:T(8,128)(2,1)}, bf16[256,2048]{1,0:T(8,128)(2,1)}, f32[8,2048]{1,0:T(8,128)}) custom-call(bf16[256,2048]{1,0:T(8,128)(2,1)} %get-tuple-element.19.in0, ...), custom_call_target="tpu_custom_call", output_to_operand_aliasing={{0}: (0, {}), {1}: (1, {}), {2}: (2, {}), {3}: (3, {})} | custom-call | tf_op jit(solution)/shard_map/second/pallas_call | solution.py:363
Async XLA Ops:
  8.5 1.6 %collective-permute-start = (bf16[2,8,16,128]{3,2,1,0:T(8,128)(2,1)S(1)}, bf16[2,8,16,128]{3,2,1,0:T(8,128)(2,1)S(1)}, u32[]{:S(2)}, u32[]{:S(2)}) collective-permute-start(bf16[2,8,16,128]{3,2,1,0:T(8,128)(2,1)S(1)} %get-tuple-element.25.sent), channel_id=1, source_target_pairs={{0,4},{4,0},{1,5},{5,1},{2,6},{6,2},{3,7},{7,3},{8,12},{12,8},{9,1... | collective-permute-start | bytes 196616 | tf_op jit(solution)/shard_map/ppermute | solution.py:362
where the time goes:
time: 15.5 us; the launch traced here: 15.3 us
  Pallas kernels  13 us (84%)
  waiting for transfers between devices  0.9 us (6%)
  starting transfers between devices  0.74 us (5%)
  between operations  0.64 us (4%)
    pallas_call x1, Pallas kernels, pair(): pl.pallas_call(functools.partial(first_kernel, shape), in_specs=[HBM] * 6...  7.84 us
    pallas_call x1, Pallas kernels, pair(): pl.pallas_call(functools.partial(second_kernel, shape), in_specs=[HBM] *...  5.19 us
    ppermute x1, waiting for transfers between devices, pair(): received = lax.ppermute(sent, 'ctx', [(0, 1), (1, 0)])  0.9 us
    ppermute x1, starting transfers between devices, pair(): received = lax.ppermute(sent, 'ctx', [(0, 1), (1, 0)])  0.74 us
  transfers between devices with their start and end apart: 1, of which 1 were waited for; matrix products, arithmetic and copies ran while one was open for 0% of the time, Pallas kernels for 0%

commit v1 on v0

--- a/solution.py
+++ b/solution.py
@@ -13,7 +13,7 @@
 GROUPS = 8
 BLOCK = GROUPS * LANES
 PAD = 8
-UNROLL = 8
+UNROLL = 16
 
 
 def one_minus_exp_2(rate, factor):
@@ -59,11 +59,18 @@
         self.chunk = min(64, length)
         self.chunks = length // self.chunk
         self.stride = length + PAD
-        self.rows = self.halves * GROUPS * self.stride
-
-
-def lanes_of(half):
-    return slice(half * BLOCK, (half + 1) * BLOCK)
+        self.plane = GROUPS * self.stride
+        self.rows = self.halves * self.plane
+
+
+def lanes_of(half, group=None):
+    if group is None:
+        return pl.ds(pl.multiple_of(half * BLOCK, BLOCK), BLOCK)
+    return pl.ds(pl.multiple_of(half * BLOCK + group * LANES, LANES), LANES)
+
+
+def groups_of(half):
+    return pl.ds(pl.multiple_of(half * GROUPS, GROUPS), GROUPS)
 
 
 def products(shape, half, token, inputs, wide):
@@ -72,11 +79,12 @@
     def body(i, carry):
         at = pl.multiple_of(token + i * step, step)
         for group in range(GROUPS):
-            lane = slice(half * BLOCK + group * LANES, half * BLOCK + (group + 1) * LANES)
-            row = pl.multiple_of((half * GROUPS + group) * shape.stride + at, 8)
-            q, dy, v, k = [inputs[j, pl.ds(at, step), lane] for j in range(4)]
-            wide[0, pl.ds(row, step), :] = (k * v).astype(F32)
-            wide[1, pl.ds(row, step), :] = (dy * q).astype(F32)
+            lane = slice(group * LANES, (group + 1) * LANES)
+            row = half * shape.plane + group * shape.stride + at
+            rows = pl.ds(pl.multiple_of(row, GROUPS), step)
+            q, dy, v, k = [inputs[j, half, pl.ds(at, step), lane] for j in range(4)]
+            wide[0, rows, :] = (k * v).astype(F32)
+            wide[1, rows, :] = (dy * q).astype(F32)
         return carry
 
     lax.fori_loop(0, shape.chunk // step, body, 0)
@@ -85,14 +93,15 @@
 def recurrence(shape, half, direction, chunk_index, factor, weight, state, dot, wide, conv):
     sign = 1 - 2 * direction
     begin = direction * (shape.length - 1) + sign * chunk_index * shape.chunk
-    base = half * GROUPS * shape.stride
+    begin = half * shape.plane + begin
+    steps = [sign * j for j in range(UNROLL)]
+    stride = sign * UNROLL
     modes = shape.modes
 
     def body(i, carry):
         state, dot = list(carry[0]), list(carry[1])
         for j in range(UNROLL):
-            row = base + begin + sign * (i * UNROLL + j)
-            rows = pl.ds(row, GROUPS, stride=shape.stride)
+            rows = pl.ds(begin + i * stride + steps[j], GROUPS, stride=shape.stride)
             source = wide[direction, rows, :]
             other = wide[1 - direction, rows, :] if dot else None
             terms = []
@@ -116,12 +125,13 @@
     def body(i, carry):
         at = pl.multiple_of(token + i * step, step)
         for group in range(GROUPS):
-            lane = slice(half * BLOCK + group * LANES, half * BLOCK + (group + 1) * LANES)
-            row = pl.multiple_of((half * GROUPS + group) * shape.stride + at, 8)
-            value = conv[pl.ds(row, step), :]
+            lane = slice(group * LANES, (group + 1) * LANES)
+            row = half * shape.plane + group * shape.stride + at
+            rows = pl.ds(pl.multiple_of(row, GROUPS), step)
+            value = conv[rows, :]
             for j in range(2):
-                staged[j, pl.ds(at, step), lane] = (
-                    inputs[2 * pair + j, pl.ds(at, step), lane].astype(F32) * value
+                staged[j, half, pl.ds(at, step), lane] = (
+                    inputs[2 * pair + j, half, pl.ds(at, step), lane].astype(F32) * value
                 ).astype(BF16)
         return carry
 
@@ -136,16 +146,16 @@
 
 
 def in_copy(shape, j, half, direction, chunk, source, inputs, sem):
-    where = (pl.ds(token_of(shape, direction, chunk), shape.chunk), lanes_of(half))
+    rows = pl.ds(token_of(shape, direction, chunk), shape.chunk)
     return pltpu.make_async_copy(
-        source.at[where], inputs.at[(j,) + where], sem.at[j, half * shape.chunks + chunk]
+        source.at[rows, lanes_of(half)], inputs.at[j, half, rows, :], sem.at[j, half * shape.chunks + chunk]
     )
 
 
 def out_copy(shape, j, half, direction, chunk, staged, target, sem):
-    where = (pl.ds(token_of(shape, direction, chunk), shape.chunk), lanes_of(half))
+    rows = pl.ds(token_of(shape, direction, chunk), shape.chunk)
     return pltpu.make_async_copy(
-        staged.at[(j,) + where], target.at[where], sem.at[j, half * shape.chunks + chunk]
+        staged.at[j, half, rows, :], target.at[rows, lanes_of(half)], sem.at[j, half * shape.chunks + chunk]
     )
 
 
@@ -167,12 +177,11 @@
 
 def first_kernel(
     shape, q, dy, v, k, rates_hbm, res_hbm,
-    out0, out1, out2, out3, wide, inputs, sent, table, scale,
-    conv, staged, rates, res, in_sem, coef_sem, out_sem,
+    conv, wide, inputs, sent, table, scale,
+    rates, res, in_sem, coef_sem,
 ):
     direction = lax.axis_index("ctx")
     sources = (q, dy, v, k)
-    targets = (out0, out1, out2, out3)
     coef = [
         pltpu.make_async_copy(rates_hbm, rates, coef_sem.at[0]),
         pltpu.make_async_copy(res_hbm, res, coef_sem.at[1]),
@@ -186,8 +195,9 @@
     for copy in coef:
         copy.wait()
     scale[...] = mode_tables(rates[...], res[...], table)
-    zero = jnp.zeros((GROUPS, LANES), F32)
-    for half in range(shape.halves):
+    zeros = (jnp.zeros((GROUPS, LANES), F32),) * shape.modes
+
+    def sweep(half, _):
         factor = table_rows(table, 0, half, shape.modes, shape.groups)
         weight = table_rows(table, 1, half, shape.modes, shape.groups)
 
@@ -199,45 +209,69 @@
             state, dot = recurrence(
                 shape, half, direction, chunk, factor, weight, carry[0], carry[1], wide, conv
             )
-            outputs(shape, half, token, direction, inputs, conv, staged)
-            send_out(shape, half, direction, direction, chunk, staged, targets, out_sem)
             return tuple(state), tuple(dot)
 
-        zeros = (zero,) * shape.modes
         state, dot = lax.fori_loop(0, shape.chunks, body, (zeros, zeros))
-        rows = slice(half * GROUPS, (half + 1) * GROUPS)
         for mode in range(shape.modes):
-            sent[0, mode, rows, :] = state[mode].astype(BF16)
-            sent[1, mode, rows, :] = dot[mode].astype(BF16)
-    wait_out(shape, direction, staged, targets, out_sem)
+            sent[0, mode, groups_of(half), :] = state[mode].astype(BF16)
+            sent[1, mode, groups_of(half), :] = dot[mode].astype(BF16)
+        return 0
+
+    lax.fori_loop(0, shape.halves, sweep, 0)
+
+
+def early_kernel(shape, conv, inputs, staged):
+    direction = lax.axis_index("ctx")
+
+    def body(i, carry):
+        half, chunk = i // shape.chunks, i % shape.chunks
+        outputs(shape, half, token_of(shape, 0, chunk), direction, inputs, conv, staged)
+        return carry
+
+    lax.fori_loop(0, shape.halves * shape.chunks, body, 0)
+
+
+def early_copy(j, half, early, target, sem):
+    return pltpu.make_async_copy(
+        early.at[j, half], target.at[:, lanes_of(half)], sem.at[j, half]
+    )
 
 
 def second_kernel(
-    shape, in0, in1, in2, in3, wide, inputs, sent, table, scale, received,
+    shape, early, wide, inputs, sent, table, scale, received,
     out0, out1, out2, out3, residue,
-    conv, staged, totals, out_sem,
+    conv, staged, totals, total, out_sem, early_sem, residue_sem,
 ):
-    del in0, in1, in2, in3
-    direction = 1 - lax.axis_index("ctx")
+    owner = lax.axis_index("ctx")
+    direction = 1 - owner
     targets = (out0, out1, out2, out3)
     modes = shape.modes
-    for half in range(shape.halves):
-        rows = slice(half * GROUPS, (half + 1) * GROUPS)
+    for p in range(2):
+
+        @pl.when(owner == p)
+        def _():
+            for j in range(2):
+                for half in range(shape.halves):
+                    early_copy(j, half, early, targets[2 * p + j], early_sem).start()
+
+    def sweep(half, _):
         factor = table_rows(table, 0, half, modes, shape.groups)
         weight = table_rows(table, 1, half, modes, shape.groups)
         state = []
         for mode in range(modes):
-            mine = sent[0, mode, rows, :].astype(F32)
-            theirs = received[0, mode, rows, :].astype(F32)
-            dots = sent[1, mode, rows, :].astype(F32) + received[1, mode, rows, :].astype(F32)
-            totals[pl.ds((half * modes + mode) * GROUPS, GROUPS), :] = (
-                dots + factor[mode] * (mine * theirs)
+            mine = sent[0, mode, groups_of(half), :].astype(F32)
+            theirs = received[0, mode, groups_of(half), :].astype(F32)
+            mine_dot = sent[1, mode, groups_of(half), :].astype(F32)
+            their_dot = received[1, mode, groups_of(half), :].astype(F32)
+            totals[pl.ds(mode * GROUPS, GROUPS), :] = (
+                mine_dot + their_dot + factor[mode] * (mine * theirs)
             )
             state.append(theirs)
         for group in range(GROUPS):
-            lane = slice(half * BLOCK + group * LANES, half * BLOCK + (group + 1) * LANES)
-            picked = totals[pl.ds(half * modes * GROUPS + group, modes, stride=GROUPS), :]
-            residue[:, lane] = picked * scale[:, lane]
+            lane = lanes_of(half, group)
+            total[:, lane] = totals[pl.ds(group, modes, stride=GROUPS), :] * scale[:, lane]
+        lane = lanes_of(half)
+        pltpu.make_async_copy(total.at[:, lane], residue.at[:, lane], residue_sem.at[half]).start()
 
         def body(chunk, state):
             token = token_of(shape, direction, chunk)
@@ -249,6 +283,15 @@
             return tuple(state)
 
         lax.fori_loop(0, shape.chunks, body, tuple(state))
+        return 0
+
+    lax.fori_loop(0, shape.halves, sweep, 0)
+    for j in range(2):
+        for half in range(shape.halves):
+            early_copy(j, half, early, targets[j], early_sem).wait()
+    for half in range(shape.halves):
+        lane = lanes_of(half)
+        pltpu.make_async_copy(total.at[:, lane], residue.at[:, lane], residue_sem.at[half]).wait()
     wait_out(shape, direction, staged, targets, out_sem)
 
 
@@ -290,7 +333,7 @@
 
         state, dot = lax.fori_loop(0, shape.chunks, forward, (zeros, zeros))
         back = lax.fori_loop(0, shape.chunks, backward, zeros)
-        rows = slice(half * GROUPS, (half + 1) * GROUPS)
+        rows = groups_of(half)
         for mode in range(shape.modes):
             ends[0, mode, rows, :] = state[mode]
             ends[1, mode, rows, :] = back[mode]
@@ -305,7 +348,7 @@
     targets = (out0, out1, out2, out3)
     for direction in range(2):
         for half in range(shape.halves):
-            rows = slice(half * GROUPS, (half + 1) * GROUPS)
+            rows = groups_of(half)
             factor = table_rows(table, 0, half, shape.modes, shape.groups)
             weight = table_rows(table, 1, half, shape.modes, shape.groups)
             state = tuple(starts[direction, mode, rows, :] for mode in range(shape.modes))
@@ -335,46 +378,53 @@
     modes, channels = shape.modes, shape.channels
     big = jax.ShapeDtypeStruct((shape.length, channels), BF16)
     copies = shape.halves * shape.chunks
-    *outs, wide, inputs, sent, table, scale = pl.pallas_call(
+    conv, wide, inputs, sent, table, scale = pl.pallas_call(
         functools.partial(first_kernel, shape),
         in_specs=[HBM] * 6,
-        out_specs=[HBM] * 4 + [VMEM] * 5,
-        out_shape=[big] * 4
-        + [
+        out_specs=[VMEM] * 6,
+        out_shape=[
+            pltpu.VMEM((shape.rows, LANES), F32),
             pltpu.VMEM((2, shape.rows, LANES), F32),
-            pltpu.VMEM((4, shape.length, channels), BF16),
+            pltpu.VMEM((4, shape.halves, shape.length, BLOCK), BF16),
             jax.ShapeDtypeStruct((2, modes, shape.groups, LANES), BF16),
             pltpu.VMEM((2 * modes * shape.groups, LANES), F32),
             pltpu.VMEM((modes, channels), F32),
         ],
         scratch_shapes=[
-            pltpu.VMEM((shape.rows, LANES), F32),
-            pltpu.VMEM((2, shape.length, channels), BF16),
             pltpu.VMEM((modes, channels), F32),
             pltpu.VMEM((modes, channels), F32),
             pltpu.SemaphoreType.DMA((4, copies)),
             pltpu.SemaphoreType.DMA((2,)),
-            pltpu.SemaphoreType.DMA((2, copies)),
         ],
         compiler_params=pltpu.CompilerParams(vmem_limit_bytes=LIMIT),
         name="first",
     )(*arrays)
     received = lax.ppermute(sent, "ctx", [(0, 1), (1, 0)])
+    early = pl.pallas_call(
+        functools.partial(early_kernel, shape),
+        in_specs=[VMEM] * 2,
+        out_specs=VMEM,
+        out_shape=pltpu.VMEM((2, shape.halves, shape.length, BLOCK), BF16),
+        compiler_params=pltpu.CompilerParams(vmem_limit_bytes=LIMIT),
+        name="early",
+    )(conv, inputs)
     *outs, residue = pl.pallas_call(
         functools.partial(second_kernel, shape),
-        in_specs=[HBM] * 4 + [VMEM] * 6,
-        out_specs=[HBM] * 4 + [VMEM],
+        in_specs=[VMEM] * 7,
+        out_specs=[HBM] * 5,
         out_shape=[big] * 4 + [jax.ShapeDtypeStruct((modes, channels), F32)],
-        input_output_aliases={0: 0, 1: 1, 2: 2, 3: 3},
         scratch_shapes=[
             pltpu.VMEM((shape.rows, LANES), F32),
-            pltpu.VMEM((2, shape.length, channels), BF16),
-            pltpu.VMEM((modes * shape.groups, LANES), F32),
+            pltpu.VMEM((2, shape.halves, shape.length, BLOCK), BF16),
+            pltpu.VMEM((modes * GROUPS, LANES), F32),
+            pltpu.VMEM((modes, channels), F32),
             pltpu.SemaphoreType.DMA((2, copies)),
+            pltpu.SemaphoreType.DMA((2, shape.halves)),
+            pltpu.SemaphoreType.DMA((shape.halves,)),
         ],
         compiler_params=pltpu.CompilerParams(vmem_limit_bytes=LIMIT),
         name="second",
-    )(*outs, wide, inputs, sent, table, scale, received)
+    )(early, wide, inputs, sent, table, scale, received)
     return outs, residue
 
 
@@ -388,7 +438,7 @@
         out_specs=[VMEM] * 5,
         out_shape=[
             pltpu.VMEM((2, shape.rows, LANES), F32),
-            pltpu.VMEM((4, shape.length, channels), BF16),
+            pltpu.VMEM((4, shape.halves, shape.length, BLOCK), BF16),
             jax.ShapeDtypeStruct((3, modes, shape.groups, LANES), F32),
             pltpu.VMEM((2 * modes * shape.groups, LANES), F32),
             jax.ShapeDtypeStruct((modes, channels), F32),
@@ -419,7 +469,7 @@
         out_shape=[big] * 4,
         scratch_shapes=[
             pltpu.VMEM((shape.rows, LANES), F32),
-            pltpu.VMEM((2, shape.length, channels), BF16),
+            pltpu.VMEM((2, shape.halves, shape.length, BLOCK), BF16),
             pltpu.SemaphoreType.DMA((2, copies)),
         ],
         compiler_params=pltpu.CompilerParams(vmem_limit_bytes=LIMIT),

time: 15.5 us -> 12.5 us (0.81)
  Pallas kernels: 13 us -> 10.7 us
  waiting for transfers between devices: 0.9 us -> 0.3 us
    pallas_call x1, Pallas kernels: 7.84 us -> 5.98 us  [pair(): pl.pallas_call(functools.partial(first_kernel, shape), in_specs=[HBM] * 6...]
    ppermute x1, waiting for transfers between devices: 0.9 us -> 0.3 us  [pair(): received = lax.ppermute(sent, 'ctx', [(0, 1), (1, 0)])]
    pallas_call x1 -> x2, Pallas kernels: 5.19 us -> 4.73 us  [the longest x1 4.13 us: pair(): pl.pallas_call(functools.partial(second_kernel, shape), in_specs=[VMEM] *...]
  transfers between devices with their start and end apart: 1 -> 1, of which waited for: 1 -> 1; matrix products, arithmetic and copies ran while one was open for 0% -> 0% of each run, Pallas kernels for 0% -> 5%
where the time goes in v1:
time: 12.5 us; the launch traced here: 12.4 us
  Pallas kernels  10.7 us (86%)
  starting transfers between devices  0.74 us (6%)
  between operations  0.65 us (5%)
  waiting for transfers between devices  0.3 us (2%)
    pallas_call x1, Pallas kernels, pair(): pl.pallas_call(functools.partial(first_kernel, shape), in_specs=[HBM] * 6...  5.98 us
    pallas_call x1, Pallas kernels, pair(): pl.pallas_call(functools.partial(second_kernel, shape), in_specs=[VMEM] *...  4.13 us
    ppermute x1, starting transfers between devices, pair(): received = lax.ppermute(sent, 'ctx', [(0, 1), (1, 0)])  0.74 us
    pallas_call x1, Pallas kernels, pair(): pl.pallas_call(functools.partial(early_kernel, shape), in_specs=[VMEM] *...  0.6 us
    ppermute x1, waiting for transfers between devices, pair(): received = lax.ppermute(sent, 'ctx', [(0, 1), (1, 0)])  0.3 us
  transfers between devices with their start and end apart: 1, of which 1 were waited for; matrix products, arithmetic and copies ran while one was open for 0% of the time, Pallas kernels for 5%

profile of v1, /device:TPU:3, one launch (start us, length us, event | category | flops | bytes accessed | tf_op | source)
XLA Modules:
  0.0 12.4 jit_solution(5991761573876020037)
XLA Ops:
  0.6 6.0 %first.1 = (f32[4224,128]{1,0:T(8,128)S(1)}, f32[2,4224,128]{2,1,0:T(8,128)S(1)}, bf16[4,2,256,1024]{3,2,1,0:T(8,128)(2,1)S(1)}, bf16[2,8,16,128]{3,2,1,0:T(8,12...) custom-call(bf16[256,2048]{1,0:T(8,128)(2,1)} %q.1, bf16[256,2048]{1,0:T(8,128)(2,1)} %dy.1, ...), custom_call_target="tpu_custom_call" | custom-call | tf_op jit(solution)/shard_map/first/pallas_call | solution.py:381
  6.6 0.7 %collective-permute-start = (bf16[2,8,16,128]{3,2,1,0:T(8,128)(2,1)S(1)}, bf16[2,8,16,128]{3,2,1,0:T(8,128)(2,1)S(1)}, u32[]{:S(2)}, u32[]{:S(2)}) collective-permute-start(bf16[2,8,16,128]{3,2,1,0:T(8,128)(2,1)S(1)} %get-tuple-element.19.sent), channel_id=1, source_target_pairs={{0,4},{4,0},{1,5},{5,1},{2,6},{6,2},{3,7},{7,3},{8,12},{12,8},{9,1... | collective-permute-start | bytes 196616 | tf_op jit(solution)/shard_map/ppermute | solution.py:402
  7.4 0.6 %early.1 = bf16[2,2,256,1024]{3,2,1,0:T(8,128)(2,1)S(1)} custom-call(f32[4224,128]{1,0:T(8,128)S(1)} %get-tuple-element.16.conv, bf16[4,2,256,1024]{3,2,1,0:T(8,128)(2,1)S(1)} %get-tuple-element.17.inputs), custom_call_target="tpu_custom_call" | custom-call | tf_op jit(solution)/shard_map/early/pallas_call | solution.py:403
  8.0 0.3 %collective-permute-done.received = bf16[2,8,16,128]{3,2,1,0:T(8,128)(2,1)S(1)} collective-permute-done((bf16[2,8,16,128]{3,2,1,0:T(8,128)(2,1)S(1)}, bf16[2,8,16,128]{3,2,1,0:T(8,128)(2,1)S(1)}, u32[]{:S(2)}, u32[]{:S(2)}) %collective-permute-start) | collective-permute-done | bytes 65568 | tf_op jit(solution)/shard_map/ppermute | solution.py:402
  8.3 4.1 %second.1 = (bf16[256,2048]{1,0:T(8,128)(2,1)}, bf16[256,2048]{1,0:T(8,128)(2,1)}, bf16[256,2048]{1,0:T(8,128)(2,1)}, bf16[256,2048]{1,0:T(8,128)(2,1)}, f32[8,2048]{1,0:T(8,128)}) custom-call(bf16[2,2,256,1024]{3,2,1,0:T(8,128)(2,1)S(1)} %early.1, f32[2,4224,128]{2,1,0:T(8,128)S(1)} %get-tuple-element.18.wide, ...), custom_call_target="tpu_custom_call" | custom-call | tf_op jit(solution)/shard_map/second/pallas_call | solution.py:411
Async XLA Ops:
  6.6 1.6 %collective-permute-start = (bf16[2,8,16,128]{3,2,1,0:T(8,128)(2,1)S(1)}, bf16[2,8,16,128]{3,2,1,0:T(8,128)(2,1)S(1)}, u32[]{:S(2)}, u32[]{:S(2)}) collective-permute-start(bf16[2,8,16,128]{3,2,1,0:T(8,128)(2,1)S(1)} %get-tuple-element.19.sent), channel_id=1, source_target_pairs={{0,4},{4,0},{1,5},{5,1},{2,6},{6,2},{3,7},{7,3},{8,12},{12,8},{9,1... | collective-permute-start | bytes 196616 | tf_op jit(solution)/shard_map/ppermute | solution.py:402

commit v2 on v1

--- a/solution.py
+++ b/solution.py
@@ -13,7 +13,7 @@
 GROUPS = 8
 BLOCK = GROUPS * LANES
 PAD = 8
-UNROLL = 16
+UNROLL = 64
 
 
 def one_minus_exp_2(rate, factor):
@@ -148,14 +148,19 @@
 def in_copy(shape, j, half, direction, chunk, source, inputs, sem):
     rows = pl.ds(token_of(shape, direction, chunk), shape.chunk)
     return pltpu.make_async_copy(
-        source.at[rows, lanes_of(half)], inputs.at[j, half, rows, :], sem.at[j, half * shape.chunks + chunk]
+        source.at[rows, lanes_of(half)], inputs.at[j, half, rows, :], sem.at[half * shape.chunks + chunk]
     )
+
+
+def in_wait(shape, half, direction, chunk, inputs, sem):
+    landed = inputs.at[:, half, pl.ds(token_of(shape, direction, chunk), shape.chunk), :]
+    pltpu.make_async_copy(landed, landed, sem.at[half * shape.chunks + chunk]).wait()
 
 
 def out_copy(shape, j, half, direction, chunk, staged, target, sem):
     rows = pl.ds(token_of(shape, direction, chunk), shape.chunk)
     return pltpu.make_async_copy(
-        staged.at[j, half, rows, :], target.at[rows, lanes_of(half)], sem.at[j, half * shape.chunks + chunk]
+        staged.at[j, half, rows, :], target.at[rows, lanes_of(half)], sem
     )
 
 
@@ -168,33 +173,29 @@
                 out_copy(shape, j, half, direction, chunk, staged, targets[2 * p + j], sem).start()
 
 
-def wait_out(shape, direction, staged, targets, sem):
-    for half in range(shape.halves):
-        for chunk in range(shape.chunks):
-            for j in range(2):
-                out_copy(shape, j, half, direction, chunk, staged, targets[j], sem).wait()
+def wait_all(array, sem):
+    pltpu.make_async_copy(array, array, sem).wait()
+
+
+def start_coefficients(rates_hbm, res_hbm, coef, sem):
+    pltpu.make_async_copy(rates_hbm, coef.at[0], sem).start()
+    pltpu.make_async_copy(res_hbm, coef.at[1], sem).start()
 
 
 def first_kernel(
     shape, q, dy, v, k, rates_hbm, res_hbm,
     conv, wide, inputs, sent, table, scale,
-    rates, res, in_sem, coef_sem,
+    coef, in_sem, coef_sem,
 ):
     direction = lax.axis_index("ctx")
     sources = (q, dy, v, k)
-    coef = [
-        pltpu.make_async_copy(rates_hbm, rates, coef_sem.at[0]),
-        pltpu.make_async_copy(res_hbm, res, coef_sem.at[1]),
-    ]
-    for copy in coef:
-        copy.start()
+    start_coefficients(rates_hbm, res_hbm, coef, coef_sem)
     for half in range(shape.halves):
         for chunk in range(shape.chunks):
             for j in range(4):
                 in_copy(shape, j, half, direction, chunk, sources[j], inputs, in_sem).start()
-    for copy in coef:
-        copy.wait()
-    scale[...] = mode_tables(rates[...], res[...], table)
+    wait_all(coef, coef_sem)
+    scale[...] = mode_tables(coef[0], coef[1], table)
     zeros = (jnp.zeros((GROUPS, LANES), F32),) * shape.modes
 
     def sweep(half, _):
@@ -203,8 +204,7 @@
 
         def body(chunk, carry):
             token = token_of(shape, direction, chunk)
-            for j in range(4):
-                in_copy(shape, j, half, direction, chunk, sources[j], inputs, in_sem).wait()
+            in_wait(shape, half, direction, chunk, inputs, in_sem)
             products(shape, half, token, inputs, wide)
             state, dot = recurrence(
                 shape, half, direction, chunk, factor, weight, carry[0], carry[1], wide, conv
@@ -233,7 +233,7 @@
 
 def early_copy(j, half, early, target, sem):
     return pltpu.make_async_copy(
-        early.at[j, half], target.at[:, lanes_of(half)], sem.at[j, half]
+        early.at[j, half], target.at[:, lanes_of(half)], sem
     )
 
 
@@ -271,7 +271,7 @@
             lane = lanes_of(half, group)
             total[:, lane] = totals[pl.ds(group, modes, stride=GROUPS), :] * scale[:, lane]
         lane = lanes_of(half)
-        pltpu.make_async_copy(total.at[:, lane], residue.at[:, lane], residue_sem.at[half]).start()
+        pltpu.make_async_copy(total.at[:, lane], residue.at[:, lane], residue_sem).start()
 
         def body(chunk, state):
             token = token_of(shape, direction, chunk)
@@ -286,41 +286,30 @@
         return 0
 
     lax.fori_loop(0, shape.halves, sweep, 0)
-    for j in range(2):
-        for half in range(shape.halves):
-            early_copy(j, half, early, targets[j], early_sem).wait()
-    for half in range(shape.halves):
-        lane = lanes_of(half)
-        pltpu.make_async_copy(total.at[:, lane], residue.at[:, lane], residue_sem.at[half]).wait()
-    wait_out(shape, direction, staged, targets, out_sem)
+    wait_all(early, early_sem)
+    wait_all(total, residue_sem)
+    wait_all(staged, out_sem)
 
 
 def ends_kernel(
     shape, q, dy, v, k, rates_hbm, res_hbm,
     wide, inputs, ends, table, scale,
-    rates, res, in_sem, coef_sem,
+    coef, in_sem, coef_sem,
 ):
     sources = (q, dy, v, k)
-    coef = [
-        pltpu.make_async_copy(rates_hbm, rates, coef_sem.at[0]),
-        pltpu.make_async_copy(res_hbm, res, coef_sem.at[1]),
-    ]
-    for copy in coef:
-        copy.start()
+    start_coefficients(rates_hbm, res_hbm, coef, coef_sem)
     for half in range(shape.halves):
         for chunk in range(shape.chunks):
             for j in range(4):
                 in_copy(shape, j, half, 0, chunk, sources[j], inputs, in_sem).start()
-    for copy in coef:
-        copy.wait()
-    scale[...] = mode_tables(rates[...], res[...], table)
+    wait_all(coef, coef_sem)
+    scale[...] = mode_tables(coef[0], coef[1], table)
     zeros = (jnp.zeros((GROUPS, LANES), F32),) * shape.modes
     for half in range(shape.halves):
         factor = table_rows(table, 0, half, shape.modes, shape.groups)
 
         def forward(chunk, carry):
-            for j in range(4):
-                in_copy(shape, j, half, 0, chunk, sources[j], inputs, in_sem).wait()
+            in_wait(shape, half, 0, chunk, inputs, in_sem)
             products(shape, half, token_of(shape, 0, chunk), inputs, wide)
             state, dot = recurrence(
                 shape, half, 0, chunk, factor, None, carry[0], carry[1], wide, None
@@ -366,7 +355,7 @@
                 return tuple(state)
 
             lax.fori_loop(0, shape.chunks, body, state)
-        wait_out(shape, direction, staged, targets[2 * direction :], out_sem)
+        wait_all(staged, out_sem)
 
 
 HBM = pl.BlockSpec(memory_space=pltpu.HBM)
@@ -391,10 +380,9 @@
             pltpu.VMEM((modes, channels), F32),
         ],
         scratch_shapes=[
-            pltpu.VMEM((modes, channels), F32),
-            pltpu.VMEM((modes, channels), F32),
-            pltpu.SemaphoreType.DMA((4, copies)),
-            pltpu.SemaphoreType.DMA((2,)),
+            pltpu.VMEM((2, modes, channels), F32),
+            pltpu.SemaphoreType.DMA((copies,)),
+            pltpu.SemaphoreType.DMA,
         ],
         compiler_params=pltpu.CompilerParams(vmem_limit_bytes=LIMIT),
         name="first",
@@ -418,9 +406,9 @@
             pltpu.VMEM((2, shape.halves, shape.length, BLOCK), BF16),
             pltpu.VMEM((modes * GROUPS, LANES), F32),
             pltpu.VMEM((modes, channels), F32),
-            pltpu.SemaphoreType.DMA((2, copies)),
-            pltpu.SemaphoreType.DMA((2, shape.halves)),
-            pltpu.SemaphoreType.DMA((shape.halves,)),
+            pltpu.SemaphoreType.DMA,
+            pltpu.SemaphoreType.DMA,
+            pltpu.SemaphoreType.DMA,
         ],
         compiler_params=pltpu.CompilerParams(vmem_limit_bytes=LIMIT),
         name="second",
@@ -444,10 +432,9 @@
             jax.ShapeDtypeStruct((modes, channels), F32),
         ],
         scratch_shapes=[
-            pltpu.VMEM((modes, channels), F32),
-            pltpu.VMEM((modes, channels), F32),
-            pltpu.SemaphoreType.DMA((4, copies)),
-            pltpu.SemaphoreType.DMA((2,)),
+            pltpu.VMEM((2, modes, channels), F32),
+            pltpu.SemaphoreType.DMA((copies,)),
+            pltpu.SemaphoreType.DMA,
         ],
         compiler_params=pltpu.CompilerParams(vmem_limit_bytes=LIMIT),
         name="ends",
@@ -470,7 +457,7 @@
         scratch_shapes=[
             pltpu.VMEM((shape.rows, LANES), F32),
             pltpu.VMEM((2, shape.halves, shape.length, BLOCK), BF16),
-            pltpu.SemaphoreType.DMA((2, copies)),
+            pltpu.SemaphoreType.DMA,
         ],
         compiler_params=pltpu.CompilerParams(vmem_limit_bytes=LIMIT),
         name="both",

time: 12.5 us -> 11.5 us (0.920)
  Pallas kernels: 10.7 us -> 9.67 us
    pallas_call x1, Pallas kernels: 5.98 us -> 5.38 us  [pair(): pl.pallas_call(functools.partial(first_kernel, shape), in_specs=[HBM] * 6...]
    pallas_call x1, Pallas kernels: 4.13 us -> 3.7 us  [pair(): pl.pallas_call(functools.partial(second_kernel, shape), in_specs=[VMEM] *...]
where the time goes in v2:
time: 11.5 us; the launch traced here: 11.4 us
  Pallas kernels  9.67 us (84%)
  starting transfers between devices  0.74 us (6%)
  between operations  0.65 us (6%)
  waiting for transfers between devices  0.3 us (3%)
    pallas_call x1, Pallas kernels, pair(): pl.pallas_call(functools.partial(first_kernel, shape), in_specs=[HBM] * 6...  5.38 us
    pallas_call x1, Pallas kernels, pair(): pl.pallas_call(functools.partial(second_kernel, shape), in_specs=[VMEM] *...  3.7 us
    ppermute x1, starting transfers between devices, pair(): received = lax.ppermute(sent, 'ctx', [(0, 1), (1, 0)])  0.74 us
    pallas_call x1, Pallas kernels, pair(): pl.pallas_call(functools.partial(early_kernel, shape), in_specs=[VMEM] *...  0.6 us
    ppermute x1, waiting for transfers between devices, pair(): received = lax.ppermute(sent, 'ctx', [(0, 1), (1, 0)])  0.3 us
  transfers between devices with their start and end apart: 1, of which 1 were waited for; matrix products, arithmetic and copies ran while one was open for 0% of the time, Pallas kernels for 5%

profile of v2, /device:TPU:3, one launch (start us, length us, event | category | flops | bytes accessed | tf_op | source)
XLA Modules:
  0.0 11.4 jit_solution(9758259547870292917)
XLA Ops:
  0.6 5.4 %first.1 = (f32[4224,128]{1,0:T(8,128)S(1)}, f32[2,4224,128]{2,1,0:T(8,128)S(1)}, bf16[4,2,256,1024]{3,2,1,0:T(8,128)(2,1)S(1)}, bf16[2,8,16,128]{3,2,1,0:T(8,12...) custom-call(bf16[256,2048]{1,0:T(8,128)(2,1)} %q.1, bf16[256,2048]{1,0:T(8,128)(2,1)} %dy.1, ...), custom_call_target="tpu_custom_call" | custom-call | tf_op jit(solution)/shard_map/first/pallas_call | solution.py:370
  6.0 0.7 %collective-permute-start = (bf16[2,8,16,128]{3,2,1,0:T(8,128)(2,1)S(1)}, bf16[2,8,16,128]{3,2,1,0:T(8,128)(2,1)S(1)}, u32[]{:S(2)}, u32[]{:S(2)}) collective-permute-start(bf16[2,8,16,128]{3,2,1,0:T(8,128)(2,1)S(1)} %get-tuple-element.19.sent), channel_id=1, source_target_pairs={{0,4},{4,0},{1,5},{5,1},{2,6},{6,2},{3,7},{7,3},{8,12},{12,8},{9,1... | collective-permute-start | bytes 196616 | tf_op jit(solution)/shard_map/ppermute | solution.py:390
  6.8 0.6 %early.1 = bf16[2,2,256,1024]{3,2,1,0:T(8,128)(2,1)S(1)} custom-call(f32[4224,128]{1,0:T(8,128)S(1)} %get-tuple-element.16.conv, bf16[4,2,256,1024]{3,2,1,0:T(8,128)(2,1)S(1)} %get-tuple-element.17.inputs), custom_call_target="tpu_custom_call" | custom-call | tf_op jit(solution)/shard_map/early/pallas_call | solution.py:391
  7.4 0.3 %collective-permute-done.received = bf16[2,8,16,128]{3,2,1,0:T(8,128)(2,1)S(1)} collective-permute-done((bf16[2,8,16,128]{3,2,1,0:T(8,128)(2,1)S(1)}, bf16[2,8,16,128]{3,2,1,0:T(8,128)(2,1)S(1)}, u32[]{:S(2)}, u32[]{:S(2)}) %collective-permute-start) | collective-permute-done | bytes 65568 | tf_op jit(solution)/shard_map/ppermute | solution.py:390
  7.7 3.7 %second.1 = (bf16[256,2048]{1,0:T(8,128)(2,1)}, bf16[256,2048]{1,0:T(8,128)(2,1)}, bf16[256,2048]{1,0:T(8,128)(2,1)}, bf16[256,2048]{1,0:T(8,128)(2,1)}, f32[8,2048]{1,0:T(8,128)}) custom-call(bf16[2,2,256,1024]{3,2,1,0:T(8,128)(2,1)S(1)} %early.1, f32[2,4224,128]{2,1,0:T(8,128)S(1)} %get-tuple-element.18.wide, ...), custom_call_target="tpu_custom_call" | custom-call | tf_op jit(solution)/shard_map/second/pallas_call | solution.py:399
Async XLA Ops:
  6.0 1.6 %collective-permute-start = (bf16[2,8,16,128]{3,2,1,0:T(8,128)(2,1)S(1)}, bf16[2,8,16,128]{3,2,1,0:T(8,128)(2,1)S(1)}, u32[]{:S(2)}, u32[]{:S(2)}) collective-permute-start(bf16[2,8,16,128]{3,2,1,0:T(8,128)(2,1)S(1)} %get-tuple-element.19.sent), channel_id=1, source_target_pairs={{0,4},{4,0},{1,5},{5,1},{2,6},{6,2},{3,7},{7,3},{8,12},{12,8},{9,1... | collective-permute-start | bytes 196616 | tf_op jit(solution)/shard_map/ppermute | solution.py:390

commit v3 on v2

--- a/solution.py
+++ b/solution.py
@@ -119,6 +119,56 @@
     return list(state), list(dot)
 
 
+def rows_of(shape, half, direction, chunk):
+    sign = 1 - 2 * direction
+    begin = half * shape.plane + direction * (shape.length - 1) + sign * chunk * shape.chunk
+    return lambda j: pl.ds(begin + sign * j, GROUPS, stride=shape.stride)
+
+
+def pair_rows(shape, half, pair, slot):
+    row = ((half * (shape.length // 2) + pair) * (shape.modes + 1) + slot) * GROUPS
+    return pl.ds(pl.multiple_of(row, GROUPS), GROUPS)
+
+
+def first_sweep(shape, half, direction, chunk, factor, weight, state, dot, rest, wide, conv, ahead):
+    rows_at = rows_of(shape, half, direction, chunk)
+    modes = shape.modes
+    state, dot = list(state), list(dot)
+    for j in range(0, shape.chunk, 2):
+        pair = chunk * (shape.chunk // 2) + j // 2
+        rows0, rows1 = rows_at(j), rows_at(j + 1)
+        source0, source1 = wide[direction, rows0, :], wide[direction, rows1, :]
+        other0, other1 = wide[1 - direction, rows0, :], wide[1 - direction, rows1, :]
+        state = [factor[mode] * state[mode] + source0 for mode in range(modes)]
+        conv[rows0, :] = tree_sum([weight[mode] * state[mode] for mode in range(modes)])
+        for mode in range(modes):
+            both = other0 + factor[mode] * other1
+            ahead[pair_rows(shape, half, pair, mode), :] = both
+            dot[mode] = dot[mode] + state[mode] * both
+        rest = rest + source1 * other1
+        ahead[pair_rows(shape, half, pair, modes), :] = other1
+        state = [factor[mode] * state[mode] + source1 for mode in range(modes)]
+        conv[rows1, :] = tree_sum([weight[mode] * state[mode] for mode in range(modes)])
+    return tuple(state), tuple(dot), rest
+
+
+def second_sweep(shape, half, direction, chunk, square, weight, weight_next, now, state, ahead, conv):
+    rows_at = rows_of(shape, half, direction, chunk)
+    modes = shape.modes
+    state = list(state)
+    for j in range(0, shape.chunk, 2):
+        pair = shape.length // 2 - 1 - chunk * (shape.chunk // 2) - j // 2
+        terms = [weight_next[mode] * state[mode] for mode in range(modes)]
+        terms.append(now * ahead[pair_rows(shape, half, pair, modes), :])
+        conv[rows_at(j), :] = tree_sum(terms)
+        state = [
+            square[mode] * state[mode] + ahead[pair_rows(shape, half, pair, mode), :]
+            for mode in range(modes)
+        ]
+        conv[rows_at(j + 1), :] = tree_sum([weight[mode] * state[mode] for mode in range(modes)])
+    return tuple(state)
+
+
 def outputs(shape, half, token, pair, inputs, conv, staged):
     step = min(32, shape.chunk)
 
@@ -184,8 +234,8 @@
 
 def first_kernel(
     shape, q, dy, v, k, rates_hbm, res_hbm,
-    conv, wide, inputs, sent, table, scale,
-    coef, in_sem, coef_sem,
+    conv, ahead, inputs, sent, table, scale,
+    wide, coef, in_sem, coef_sem,
 ):
     direction = lax.axis_index("ctx")
     sources = (q, dy, v, k)
@@ -198,26 +248,29 @@
     scale[...] = mode_tables(coef[0], coef[1], table)
     zeros = (jnp.zeros((GROUPS, LANES), F32),) * shape.modes
 
-    def sweep(half, _):
-        factor = table_rows(table, 0, half, shape.modes, shape.groups)
-        weight = table_rows(table, 1, half, shape.modes, shape.groups)
-
-        def body(chunk, carry):
-            token = token_of(shape, direction, chunk)
-            in_wait(shape, half, direction, chunk, inputs, in_sem)
-            products(shape, half, token, inputs, wide)
-            state, dot = recurrence(
-                shape, half, direction, chunk, factor, weight, carry[0], carry[1], wide, conv
-            )
-            return tuple(state), tuple(dot)
-
-        state, dot = lax.fori_loop(0, shape.chunks, body, (zeros, zeros))
-        for mode in range(shape.modes):
-            sent[0, mode, groups_of(half), :] = state[mode].astype(BF16)
-            sent[1, mode, groups_of(half), :] = dot[mode].astype(BF16)
-        return 0
-
-    lax.fori_loop(0, shape.halves, sweep, 0)
+    def run(way):
+        def sweep(half, _):
+            factor = table_rows(table, 0, half, shape.modes, shape.groups)
+            weight = table_rows(table, 1, half, shape.modes, shape.groups)
+
+            def body(chunk, carry):
+                token = token_of(shape, way, chunk)
+                in_wait(shape, half, way, chunk, inputs, in_sem)
+                products(shape, half, token, inputs, wide)
+                return first_sweep(
+                    shape, half, way, chunk, factor, weight, *carry, wide, conv, ahead
+                )
+
+            state, dot, rest = lax.fori_loop(0, shape.chunks, body, (zeros, zeros, zeros[0]))
+            for mode in range(shape.modes):
+                sent[0, mode, groups_of(half), :] = state[mode].astype(BF16)
+                sent[1, mode, groups_of(half), :] = (dot[mode] + rest).astype(BF16)
+            return 0
+
+        lax.fori_loop(0, shape.halves, sweep, 0)
+
+    for way in range(2):
+        pl.when(direction == way)(functools.partial(run, way))
 
 
 def early_kernel(shape, conv, inputs, staged):
@@ -238,7 +291,7 @@
 
 
 def second_kernel(
-    shape, early, wide, inputs, sent, table, scale, received,
+    shape, early, ahead, inputs, sent, table, scale, received,
     out0, out1, out2, out3, residue,
     conv, staged, totals, total, out_sem, early_sem, residue_sem,
 ):
@@ -254,38 +307,49 @@
                 for half in range(shape.halves):
                     early_copy(j, half, early, targets[2 * p + j], early_sem).start()
 
-    def sweep(half, _):
-        factor = table_rows(table, 0, half, modes, shape.groups)
-        weight = table_rows(table, 1, half, modes, shape.groups)
-        state = []
-        for mode in range(modes):
-            mine = sent[0, mode, groups_of(half), :].astype(F32)
-            theirs = received[0, mode, groups_of(half), :].astype(F32)
-            mine_dot = sent[1, mode, groups_of(half), :].astype(F32)
-            their_dot = received[1, mode, groups_of(half), :].astype(F32)
-            totals[pl.ds(mode * GROUPS, GROUPS), :] = (
-                mine_dot + their_dot + factor[mode] * (mine * theirs)
-            )
-            state.append(theirs)
-        for group in range(GROUPS):
-            lane = lanes_of(half, group)
-            total[:, lane] = totals[pl.ds(group, modes, stride=GROUPS), :] * scale[:, lane]
-        lane = lanes_of(half)
-        pltpu.make_async_copy(total.at[:, lane], residue.at[:, lane], residue_sem).start()
-
-        def body(chunk, state):
-            token = token_of(shape, direction, chunk)
-            state, _ = recurrence(
-                shape, half, direction, chunk, factor, weight, state, (), wide, conv
-            )
-            outputs(shape, half, token, direction, inputs, conv, staged)
-            send_out(shape, half, direction, direction, chunk, staged, targets, out_sem)
-            return tuple(state)
-
-        lax.fori_loop(0, shape.chunks, body, tuple(state))
-        return 0
-
-    lax.fori_loop(0, shape.halves, sweep, 0)
+    def run(way):
+        def sweep(half, _):
+            factor = table_rows(table, 0, half, modes, shape.groups)
+            weight = table_rows(table, 1, half, modes, shape.groups)
+            square = [value * value for value in factor]
+            weight_next = [weight[mode] * factor[mode] for mode in range(modes)]
+            now = tree_sum(weight)
+            state = []
+            for mode in range(modes):
+                mine = sent[0, mode, groups_of(half), :].astype(F32)
+                theirs = received[0, mode, groups_of(half), :].astype(F32)
+                mine_dot = sent[1, mode, groups_of(half), :].astype(F32)
+                their_dot = received[1, mode, groups_of(half), :].astype(F32)
+                totals[pl.ds(mode * GROUPS, GROUPS), :] = (
+                    mine_dot + their_dot + factor[mode] * (mine * theirs)
+                )
+                state.append(theirs)
+            for group in range(GROUPS):
+                lane = lanes_of(half, group)
+                total[:, lane] = totals[pl.ds(group, modes, stride=GROUPS), :] * scale[:, lane]
+            lane = lanes_of(half)
+            pltpu.make_async_copy(total.at[:, lane], residue.at[:, lane], residue_sem).start()
+
+            def body(chunk, state):
+                token = token_of(shape, way, chunk)
+                state = second_sweep(
+                    shape, half, way, chunk, square, weight, weight_next, now, state, ahead, conv
+                )
+                outputs(shape, half, token, way, inputs, conv, staged)
+                for j in range(2):
+                    out_copy(
+                        shape, j, half, way, chunk, staged, targets[2 * way + j], out_sem
+                    ).start()
+                return state
+
+            lax.fori_loop(0, shape.chunks, body, tuple(state))
+            return 0
+
+        lax.fori_loop(0, shape.halves, sweep, 0)
+
+    for way in range(2):
+        pl.when(direction == way)(functools.partial(run, way))
+
     wait_all(early, early_sem)
     wait_all(total, residue_sem)
     wait_all(staged, out_sem)
@@ -367,19 +431,20 @@
     modes, channels = shape.modes, shape.channels
     big = jax.ShapeDtypeStruct((shape.length, channels), BF16)
     copies = shape.halves * shape.chunks
-    conv, wide, inputs, sent, table, scale = pl.pallas_call(
+    conv, ahead, inputs, sent, table, scale = pl.pallas_call(
         functools.partial(first_kernel, shape),
         in_specs=[HBM] * 6,
         out_specs=[VMEM] * 6,
         out_shape=[
             pltpu.VMEM((shape.rows, LANES), F32),
-            pltpu.VMEM((2, shape.rows, LANES), F32),
+            pltpu.VMEM((shape.groups * shape.length // 2 * (modes + 1), LANES), F32),
             pltpu.VMEM((4, shape.halves, shape.length, BLOCK), BF16),
             jax.ShapeDtypeStruct((2, modes, shape.groups, LANES), BF16),
             pltpu.VMEM((2 * modes * shape.groups, LANES), F32),
             pltpu.VMEM((modes, channels), F32),
         ],
         scratch_shapes=[
+            pltpu.VMEM((2, shape.rows, LANES), F32),
             pltpu.VMEM((2, modes, channels), F32),
             pltpu.SemaphoreType.DMA((copies,)),
             pltpu.SemaphoreType.DMA,
@@ -412,7 +477,7 @@
         ],
         compiler_params=pltpu.CompilerParams(vmem_limit_bytes=LIMIT),
         name="second",
-    )(early, wide, inputs, sent, table, scale, received)
+    )(early, ahead, inputs, sent, table, scale, received)
     return outs, residue
 
 

time: 11.5 us -> 11 us (0.957)
  Pallas kernels: 9.67 us -> 9.17 us
    pallas_call x1, Pallas kernels: 3.7 us -> 3.08 us  [pair(): pl.pallas_call(functools.partial(second_kernel, shape), in_specs=[VMEM] *...]
where the time goes in v3:
time: 11 us; the launch traced here: 10.9 us
  Pallas kernels  9.17 us (83%)
  starting transfers between devices  0.74 us (7%)
  between operations  0.65 us (6%)
  waiting for transfers between devices  0.3 us (3%)
    pallas_call x1, Pallas kernels, pair(): pl.pallas_call(functools.partial(first_kernel, shape), in_specs=[HBM] * 6...  5.49 us
    pallas_call x1, Pallas kernels, pair(): pl.pallas_call(functools.partial(second_kernel, shape), in_specs=[VMEM] *...  3.08 us
    ppermute x1, starting transfers between devices, pair(): received = lax.ppermute(sent, 'ctx', [(0, 1), (1, 0)])  0.74 us
    pallas_call x1, Pallas kernels, pair(): pl.pallas_call(functools.partial(early_kernel, shape), in_specs=[VMEM] *...  0.6 us
    ppermute x1, waiting for transfers between devices, pair(): received = lax.ppermute(sent, 'ctx', [(0, 1), (1, 0)])  0.3 us
  transfers between devices with their start and end apart: 1, of which 1 were waited for; matrix products, arithmetic and copies ran while one was open for 0% of the time, Pallas kernels for 5%

profile of v3, /device:TPU:3, one launch (start us, length us, event | category | flops | bytes accessed | tf_op | source)
XLA Modules:
  0.0 10.9 jit_solution(9909033296509230225)
XLA Ops:
  0.6 5.5 %first.1 = (f32[4224,128]{1,0:T(8,128)S(1)}, f32[18432,128]{1,0:T(8,128)S(1)}, bf16[4,2,256,1024]{3,2,1,0:T(8,128)(2,1)S(1)}, bf16[2,8,16,128]{3,2,1,0:T(8,128)(...) custom-call(bf16[256,2048]{1,0:T(8,128)(2,1)} %q.1, bf16[256,2048]{1,0:T(8,128)(2,1)} %dy.1, ...), custom_call_target="tpu_custom_call" | custom-call | tf_op jit(solution)/shard_map/first/pallas_call | solution.py:434
  6.1 0.7 %collective-permute-start = (bf16[2,8,16,128]{3,2,1,0:T(8,128)(2,1)S(1)}, bf16[2,8,16,128]{3,2,1,0:T(8,128)(2,1)S(1)}, u32[]{:S(2)}, u32[]{:S(2)}) collective-permute-start(bf16[2,8,16,128]{3,2,1,0:T(8,128)(2,1)S(1)} %get-tuple-element.19.sent), channel_id=1, source_target_pairs={{0,4},{4,0},{1,5},{5,1},{2,6},{6,2},{3,7},{7,3},{8,12},{12,8},{9,1... | collective-permute-start | bytes 196616 | tf_op jit(solution)/shard_map/ppermute | solution.py:455
  6.9 0.6 %early.1 = bf16[2,2,256,1024]{3,2,1,0:T(8,128)(2,1)S(1)} custom-call(f32[4224,128]{1,0:T(8,128)S(1)} %get-tuple-element.16.conv, bf16[4,2,256,1024]{3,2,1,0:T(8,128)(2,1)S(1)} %get-tuple-element.17.inputs), custom_call_target="tpu_custom_call" | custom-call | tf_op jit(solution)/shard_map/early/pallas_call | solution.py:456
  7.5 0.3 %collective-permute-done.received = bf16[2,8,16,128]{3,2,1,0:T(8,128)(2,1)S(1)} collective-permute-done((bf16[2,8,16,128]{3,2,1,0:T(8,128)(2,1)S(1)}, bf16[2,8,16,128]{3,2,1,0:T(8,128)(2,1)S(1)}, u32[]{:S(2)}, u32[]{:S(2)}) %collective-permute-start) | collective-permute-done | bytes 65568 | tf_op jit(solution)/shard_map/ppermute | solution.py:455
  7.8 3.1 %second.1 = (bf16[256,2048]{1,0:T(8,128)(2,1)}, bf16[256,2048]{1,0:T(8,128)(2,1)}, bf16[256,2048]{1,0:T(8,128)(2,1)}, bf16[256,2048]{1,0:T(8,128)(2,1)}, f32[8,2048]{1,0:T(8,128)}) custom-call(bf16[2,2,256,1024]{3,2,1,0:T(8,128)(2,1)S(1)} %early.1, f32[18432,128]{1,0:T(8,128)S(1)} %get-tuple-element.18.ahead, ...), custom_call_target="tpu_custom_call" | custom-call | tf_op jit(solution)/shard_map/second/pallas_call | solution.py:464
Async XLA Ops:
  6.1 1.6 %collective-permute-start = (bf16[2,8,16,128]{3,2,1,0:T(8,128)(2,1)S(1)}, bf16[2,8,16,128]{3,2,1,0:T(8,128)(2,1)S(1)}, u32[]{:S(2)}, u32[]{:S(2)}) collective-permute-start(bf16[2,8,16,128]{3,2,1,0:T(8,128)(2,1)S(1)} %get-tuple-element.19.sent), channel_id=1, source_target_pairs={{0,4},{4,0},{1,5},{5,1},{2,6},{6,2},{3,7},{7,3},{8,12},{12,8},{9,1... | collective-permute-start | bytes 196616 | tf_op jit(solution)/shard_map/ppermute | solution.py:455

commit v4 on v3

--- a/solution.py
+++ b/solution.py
@@ -130,17 +130,54 @@
     return pl.ds(pl.multiple_of(row, GROUPS), GROUPS)
 
 
-def first_sweep(shape, half, direction, chunk, factor, weight, state, dot, rest, wide, conv, ahead):
+def held_rows(shape, half, j, mode):
+    row = ((half * shape.chunk + j) * shape.modes + mode) * GROUPS
+    return pl.ds(pl.multiple_of(row, GROUPS), GROUPS)
+
+
+def near_products(shape, half, direction, chunk, index, inputs, near):
+    start = shape.chunk - 8 - 8 * index if direction else 8 * index
+    at = pl.multiple_of(token_of(shape, direction, chunk) + start, 8)
+    first, second = 2 * (1 - direction), 2 * direction
+    for group in range(GROUPS):
+        lane = slice(group * LANES, (group + 1) * LANES)
+        rows = pl.ds(group * (shape.chunk + PAD) + start, 8)
+        a0, a1, b0, b1 = [
+            inputs[plane + j, half, pl.ds(at, 8), lane] for plane in (first, second) for j in range(2)
+        ]
+        near[0, rows, :] = (a0 * a1).astype(F32)
+        near[1, rows, :] = (b0 * b1).astype(F32)
+
+
+def first_sweep(
+    shape, half, direction, chunk, coming, factor, weight, state, dot, rest,
+    inputs, near, conv, ahead, held,
+):
     rows_at = rows_of(shape, half, direction, chunk)
     modes = shape.modes
     state, dot = list(state), list(dot)
+
+    def emit(j, state):
+        if weight is not None:
+            conv[rows_at(j), :] = tree_sum([weight[mode] * state[mode] for mode in range(modes)])
+            return
+        for mode in range(modes):
+            held[held_rows(shape, half, j, mode), :] = state[mode]
+
+    def near_row(j):
+        token = shape.chunk - 1 - j if direction else j
+        return pl.ds(token, GROUPS, stride=shape.chunk + PAD)
+
     for j in range(0, shape.chunk, 2):
+        if j % 8 == 0:
+            index = j // 8 + 1
+            if index < shape.chunk // 8:
+                near_products(shape, half, direction, chunk, index, inputs, near)
         pair = chunk * (shape.chunk // 2) + j // 2
-        rows0, rows1 = rows_at(j), rows_at(j + 1)
-        source0, source1 = wide[direction, rows0, :], wide[direction, rows1, :]
-        other0, other1 = wide[1 - direction, rows0, :], wide[1 - direction, rows1, :]
+        source0, source1 = near[0, near_row(j), :], near[0, near_row(j + 1), :]
+        other0, other1 = near[1, near_row(j), :], near[1, near_row(j + 1), :]
         state = [factor[mode] * state[mode] + source0 for mode in range(modes)]
-        conv[rows0, :] = tree_sum([weight[mode] * state[mode] for mode in range(modes)])
+        emit(j, state)
         for mode in range(modes):
             both = other0 + factor[mode] * other1
             ahead[pair_rows(shape, half, pair, mode), :] = both
@@ -148,7 +185,8 @@
         rest = rest + source1 * other1
         ahead[pair_rows(shape, half, pair, modes), :] = other1
         state = [factor[mode] * state[mode] + source1 for mode in range(modes)]
-        conv[rows1, :] = tree_sum([weight[mode] * state[mode] for mode in range(modes)])
+        emit(j + 1, state)
+    near_products(shape, *coming, inputs, near)
     return tuple(state), tuple(dot), rest
 
 
@@ -234,8 +272,8 @@
 
 def first_kernel(
     shape, q, dy, v, k, rates_hbm, res_hbm,
-    conv, ahead, inputs, sent, table, scale,
-    wide, coef, in_sem, coef_sem,
+    conv, ahead, held, inputs, sent, table, scale,
+    near, coef, in_sem, coef_sem,
 ):
     direction = lax.axis_index("ctx")
     sources = (q, dy, v, k)
@@ -248,20 +286,32 @@
     scale[...] = mode_tables(coef[0], coef[1], table)
     zeros = (jnp.zeros((GROUPS, LANES), F32),) * shape.modes
 
+    items = shape.halves * shape.chunks
+
     def run(way):
+        in_wait(shape, 0, way, 0, inputs, in_sem)
+        near_products(shape, 0, way, 0, 0, inputs, near)
+
         def sweep(half, _):
             factor = table_rows(table, 0, half, shape.modes, shape.groups)
             weight = table_rows(table, 1, half, shape.modes, shape.groups)
 
-            def body(chunk, carry):
-                token = token_of(shape, way, chunk)
-                in_wait(shape, half, way, chunk, inputs, in_sem)
-                products(shape, half, token, inputs, wide)
+            def body(chunk, carry, weight=weight):
+                item = half * shape.chunks + chunk + 1
+                coming = jnp.minimum(item, items - 1)
+                coming = (coming // shape.chunks, way, coming % shape.chunks)
+
+                @pl.when(item < items)
+                def _():
+                    in_wait(shape, *coming, inputs, in_sem)
+
                 return first_sweep(
-                    shape, half, way, chunk, factor, weight, *carry, wide, conv, ahead
+                    shape, half, way, chunk, (*coming, 0), factor, weight, *carry,
+                    inputs, near, conv, ahead, held,
                 )
 
-            state, dot, rest = lax.fori_loop(0, shape.chunks, body, (zeros, zeros, zeros[0]))
+            carry = lax.fori_loop(0, shape.chunks - 1, body, (zeros, zeros, zeros[0]))
+            state, dot, rest = body(shape.chunks - 1, carry, None)
             for mode in range(shape.modes):
                 sent[0, mode, groups_of(half), :] = state[mode].astype(BF16)
                 sent[1, mode, groups_of(half), :] = (dot[mode] + rest).astype(BF16)
@@ -273,8 +323,29 @@
         pl.when(direction == way)(functools.partial(run, way))
 
 
-def early_kernel(shape, conv, inputs, staged):
+def early_kernel(shape, conv_in, held, inputs, table, conv, staged):
+    del conv_in
     direction = lax.axis_index("ctx")
+    step = 16
+
+    def last(half, carry):
+        weight = table_rows(table, 1, half, shape.modes, shape.groups)
+        rows_at = rows_of(shape, half, direction, shape.chunks - 1)
+
+        def tokens(i, carry):
+            for k in range(step):
+                j = i * step + k
+                conv[rows_at(j), :] = tree_sum(
+                    [
+                        weight[mode] * held[held_rows(shape, half, j, mode), :]
+                        for mode in range(shape.modes)
+                    ]
+                )
+            return carry
+
+        return lax.fori_loop(0, shape.chunk // step, tokens, carry)
+
+    lax.fori_loop(0, shape.halves, last, 0)
 
     def body(i, carry):
         half, chunk = i // shape.chunks, i % shape.chunks
@@ -431,20 +502,21 @@
     modes, channels = shape.modes, shape.channels
     big = jax.ShapeDtypeStruct((shape.length, channels), BF16)
     copies = shape.halves * shape.chunks
-    conv, ahead, inputs, sent, table, scale = pl.pallas_call(
+    conv, ahead, held, inputs, sent, table, scale = pl.pallas_call(
         functools.partial(first_kernel, shape),
         in_specs=[HBM] * 6,
-        out_specs=[VMEM] * 6,
+        out_specs=[VMEM] * 7,
         out_shape=[
             pltpu.VMEM((shape.rows, LANES), F32),
             pltpu.VMEM((shape.groups * shape.length // 2 * (modes + 1), LANES), F32),
+            pltpu.VMEM((shape.groups * shape.chunk * modes, LANES), F32),
             pltpu.VMEM((4, shape.halves, shape.length, BLOCK), BF16),
             jax.ShapeDtypeStruct((2, modes, shape.groups, LANES), BF16),
             pltpu.VMEM((2 * modes * shape.groups, LANES), F32),
             pltpu.VMEM((modes, channels), F32),
         ],
         scratch_shapes=[
-            pltpu.VMEM((2, shape.rows, LANES), F32),
+            pltpu.VMEM((2, (shape.chunk + PAD) * GROUPS, LANES), F32),
             pltpu.VMEM((2, modes, channels), F32),
             pltpu.SemaphoreType.DMA((copies,)),
             pltpu.SemaphoreType.DMA,
@@ -453,14 +525,18 @@
         name="first",
     )(*arrays)
     received = lax.ppermute(sent, "ctx", [(0, 1), (1, 0)])
-    early = pl.pallas_call(
+    _, early = pl.pallas_call(
         functools.partial(early_kernel, shape),
-        in_specs=[VMEM] * 2,
-        out_specs=VMEM,
-        out_shape=pltpu.VMEM((2, shape.halves, shape.length, BLOCK), BF16),
+        in_specs=[VMEM] * 4,
+        out_specs=[VMEM] * 2,
+        out_shape=[
+            pltpu.VMEM((shape.rows, LANES), F32),
+            pltpu.VMEM((2, shape.halves, shape.length, BLOCK), BF16),
+        ],
+        input_output_aliases={0: 0},
         compiler_params=pltpu.CompilerParams(vmem_limit_bytes=LIMIT),
         name="early",
-    )(conv, inputs)
+    )(conv, held, inputs, table)
     *outs, residue = pl.pallas_call(
         functools.partial(second_kernel, shape),
         in_specs=[VMEM] * 7,

time: 11 us -> 10.8 us (0.982)
  waiting for transfers between devices: 0.3 us -> 0.01 us
    pallas_call x1, Pallas kernels: 0.6 us -> 0.94 us  [pair(): pl.pallas_call(functools.partial(early_kernel, shape), in_specs=[VMEM] *...]
    pallas_call x1, Pallas kernels: 5.49 us -> 5.2 us  [pair(): pl.pallas_call(functools.partial(first_kernel, shape), in_specs=[HBM] * 6...]
    ppermute x1, waiting for transfers between devices: 0.3 us -> 0.01 us  [pair(): received = lax.ppermute(sent, 'ctx', [(0, 1), (1, 0)])]
  transfers between devices with their start and end apart: 1 -> 1, of which waited for: 1 -> 0; matrix products, arithmetic and copies ran while one was open for 0% -> 0% of each run, Pallas kernels for 5% -> 9%
where the time goes in v4:
time: 10.8 us; the launch traced here: 10.6 us
  Pallas kernels  9.24 us (86%)
  starting transfers between devices  0.73 us (7%)
  between operations  0.66 us (6%)
    pallas_call x1, Pallas kernels, pair(): pl.pallas_call(functools.partial(first_kernel, shape), in_specs=[HBM] * 6...  5.2 us
    pallas_call x1, Pallas kernels, pair(): pl.pallas_call(functools.partial(second_kernel, shape), in_specs=[VMEM] *...  3.11 us
    pallas_call x1, Pallas kernels, pair(): pl.pallas_call(functools.partial(early_kernel, shape), in_specs=[VMEM] *...  0.94 us
    ppermute x1, starting transfers between devices, pair(): received = lax.ppermute(sent, 'ctx', [(0, 1), (1, 0)])  0.73 us
  transfers between devices with their start and end apart: 1, of which 0 were waited for; matrix products, arithmetic and copies ran while one was open for 0% of the time, Pallas kernels for 9%

profile of v4, /device:TPU:3, one launch (start us, length us, event | category | flops | bytes accessed | tf_op | source)
XLA Modules:
  0.0 10.6 jit_solution(18095660435478885451)
XLA Ops:
  0.6 5.2 %first.1 = (f32[4224,128]{1,0:T(8,128)S(1)}, f32[18432,128]{1,0:T(8,128)S(1)}, f32[8192,128]{1,0:T(8,128)S(1)}, bf16[4,2,256,1024]{3,2,1,0:T(8,128)(2,1)S(1)}, b...) custom-call(bf16[256,2048]{1,0:T(8,128)(2,1)} %q.1, bf16[256,2048]{1,0:T(8,128)(2,1)} %dy.1, ...), custom_call_target="tpu_custom_call" | custom-call | tf_op jit(solution)/shard_map/first/pallas_call | solution.py:505
  5.8 0.7 %collective-permute-start = (bf16[2,8,16,128]{3,2,1,0:T(8,128)(2,1)S(1)}, bf16[2,8,16,128]{3,2,1,0:T(8,128)(2,1)S(1)}, u32[]{:S(2)}, u32[]{:S(2)}) collective-permute-start(bf16[2,8,16,128]{3,2,1,0:T(8,128)(2,1)S(1)} %get-tuple-element.24.sent), channel_id=1, source_target_pairs={{0,4},{4,0},{1,5},{5,1},{2,6},{6,2},{3,7},{7,3},{8,12},{12,8},{9,1... | collective-permute-start | bytes 196616 | tf_op jit(solution)/shard_map/ppermute | solution.py:527
  6.6 0.9 %early.1 = (f32[4224,128]{1,0:T(8,128)S(1)}, bf16[2,2,256,1024]{3,2,1,0:T(8,128)(2,1)S(1)}) custom-call(f32[4224,128]{1,0:T(8,128)S(1)} %get-tuple-element.18.conv_in, f32[8192,128]{1,0:T(8,128)S(1)} %get-tuple-element.19.held, bf16[4,2,256,1024]{3,2,1,0:T(8,128)(2,1)S(1)} %get-tuple-element.20.inputs, ...), custom_call_target="tpu_custom_call", output_to_operand_aliasing={{0}: (0, {})} | custom-call | tf_op jit(solution)/shard_map/early/pallas_call | solution.py:528
  7.5 0.0 collective-permute-done.received
  7.5 3.1 %second.1 = (bf16[256,2048]{1,0:T(8,128)(2,1)}, bf16[256,2048]{1,0:T(8,128)(2,1)}, bf16[256,2048]{1,0:T(8,128)(2,1)}, bf16[256,2048]{1,0:T(8,128)(2,1)}, f32[8,2048]{1,0:T(8,128)}) custom-call(bf16[2,2,256,1024]{3,2,1,0:T(8,128)(2,1)S(1)} %get-tuple-element.22.early, f32[18432,128]{1,0:T(8,128)S(1)} %get-tuple-element.23.ahead, ...), custom_call_target="tpu_custom_call" | custom-call | tf_op jit(solution)/shard_map/second/pallas_call | solution.py:540
Async XLA Ops:
  5.8 1.7 %collective-permute-start = (bf16[2,8,16,128]{3,2,1,0:T(8,128)(2,1)S(1)}, bf16[2,8,16,128]{3,2,1,0:T(8,128)(2,1)S(1)}, u32[]{:S(2)}, u32[]{:S(2)}) collective-permute-start(bf16[2,8,16,128]{3,2,1,0:T(8,128)(2,1)S(1)} %get-tuple-element.24.sent), channel_id=1, source_target_pairs={{0,4},{4,0},{1,5},{5,1},{2,6},{6,2},{3,7},{7,3},{8,12},{12,8},{9,1... | collective-permute-start | bytes 196616 | tf_op jit(solution)/shard_map/ppermute | solution.py:527

commit v5 on v4

--- a/solution.py
+++ b/solution.py
@@ -245,6 +245,21 @@
     pltpu.make_async_copy(landed, landed, sem.at[half * shape.chunks + chunk]).wait()
 
 
+def split_rows(shape, direction):
+    half, chunk = 1 // shape.chunks, 1 % shape.chunks
+    token = token_of(shape, direction, chunk)
+    head = pl.multiple_of(token + direction * (shape.chunk - 8), 8)
+    rest = pl.multiple_of(token + (1 - direction) * 8, 8)
+    return half, pl.ds(head, 8), pl.ds(rest, shape.chunk - 8)
+
+
+def split_wait(shape, direction, which, inputs, sem):
+    half, *parts = split_rows(shape, direction)
+    landed = inputs.at[:, half, parts[which], :]
+    index = shape.halves * shape.chunks if which else 1
+    pltpu.make_async_copy(landed, landed, sem.at[index]).wait()
+
+
 def out_copy(shape, j, half, direction, chunk, staged, target, sem):
     rows = pl.ds(token_of(shape, direction, chunk), shape.chunk)
     return pltpu.make_async_copy(
@@ -278,15 +293,24 @@
     direction = lax.axis_index("ctx")
     sources = (q, dy, v, k)
     start_coefficients(rates_hbm, res_hbm, coef, coef_sem)
-    for half in range(shape.halves):
-        for chunk in range(shape.chunks):
-            for j in range(4):
-                in_copy(shape, j, half, direction, chunk, sources[j], inputs, in_sem).start()
+    items = shape.halves * shape.chunks
+    for item in range(items):
+        if item == 1:
+            half, *parts = split_rows(shape, direction)
+            for tokens, index in zip(parts, (1, items)):
+                for j in range(4):
+                    pltpu.make_async_copy(
+                        sources[j].at[tokens, lanes_of(half)],
+                        inputs.at[j, half, tokens, :],
+                        in_sem.at[index],
+                    ).start()
+            continue
+        half, chunk = item // shape.chunks, item % shape.chunks
+        for j in range(4):
+            in_copy(shape, j, half, direction, chunk, sources[j], inputs, in_sem).start()
     wait_all(coef, coef_sem)
     scale[...] = mode_tables(coef[0], coef[1], table)
     zeros = (jnp.zeros((GROUPS, LANES), F32),) * shape.modes
-
-    items = shape.halves * shape.chunks
 
     def run(way):
         in_wait(shape, 0, way, 0, inputs, in_sem)
@@ -301,9 +325,14 @@
                 coming = jnp.minimum(item, items - 1)
                 coming = (coming // shape.chunks, way, coming % shape.chunks)
 
-                @pl.when(item < items)
+                @pl.when((item < items) & (item != 1))
                 def _():
                     in_wait(shape, *coming, inputs, in_sem)
+
+                for which in range(2):
+                    pl.when(item == 1 + which)(
+                        functools.partial(split_wait, shape, way, which, inputs, in_sem)
+                    )
 
                 return first_sweep(
                     shape, half, way, chunk, (*coming, 0), factor, weight, *carry,
@@ -518,7 +547,7 @@
         scratch_shapes=[
             pltpu.VMEM((2, (shape.chunk + PAD) * GROUPS, LANES), F32),
             pltpu.VMEM((2, modes, channels), F32),
-            pltpu.SemaphoreType.DMA((copies,)),
+            pltpu.SemaphoreType.DMA((copies + 1,)),
             pltpu.SemaphoreType.DMA,
         ],
         compiler_params=pltpu.CompilerParams(vmem_limit_bytes=LIMIT),

time: 10.8 us -> 10.7 us (level)
  no operation moved by 1% of the time
where the time goes in v5:
time: 10.7 us; the launch traced here: 10.5 us
  Pallas kernels  9.15 us (86%)
  starting transfers between devices  0.73 us (7%)
  between operations  0.66 us (6%)
    pallas_call x1, Pallas kernels, pair(): pl.pallas_call(functools.partial(first_kernel, shape), in_specs=[HBM] * 6...  5.1 us
    pallas_call x1, Pallas kernels, pair(): pl.pallas_call(functools.partial(second_kernel, shape), in_specs=[VMEM] *...  3.11 us
    pallas_call x1, Pallas kernels, pair(): pl.pallas_call(functools.partial(early_kernel, shape), in_specs=[VMEM] *...  0.94 us
    ppermute x1, starting transfers between devices, pair(): received = lax.ppermute(sent, 'ctx', [(0, 1), (1, 0)])  0.73 us
  transfers between devices with their start and end apart: 1, of which 0 were waited for; matrix products, arithmetic and copies ran while one was open for 0% of the time, Pallas kernels for 9%

profile of v5, /device:TPU:3, one launch (start us, length us, event | category | flops | bytes accessed | tf_op | source)
XLA Modules:
  0.0 10.5 jit_solution(10995896838009532685)
XLA Ops:
  0.6 5.1 %first.1 = (f32[4224,128]{1,0:T(8,128)S(1)}, f32[18432,128]{1,0:T(8,128)S(1)}, f32[8192,128]{1,0:T(8,128)S(1)}, bf16[4,2,256,1024]{3,2,1,0:T(8,128)(2,1)S(1)}, b...) custom-call(bf16[256,2048]{1,0:T(8,128)(2,1)} %q.1, bf16[256,2048]{1,0:T(8,128)(2,1)} %dy.1, ...), custom_call_target="tpu_custom_call" | custom-call | tf_op jit(solution)/shard_map/first/pallas_call | solution.py:534
  5.7 0.7 %collective-permute-start = (bf16[2,8,16,128]{3,2,1,0:T(8,128)(2,1)S(1)}, bf16[2,8,16,128]{3,2,1,0:T(8,128)(2,1)S(1)}, u32[]{:S(2)}, u32[]{:S(2)}) collective-permute-start(bf16[2,8,16,128]{3,2,1,0:T(8,128)(2,1)S(1)} %get-tuple-element.24.sent), channel_id=1, source_target_pairs={{0,4},{4,0},{1,5},{5,1},{2,6},{6,2},{3,7},{7,3},{8,12},{12,8},{9,1... | collective-permute-start | bytes 196616 | tf_op jit(solution)/shard_map/ppermute | solution.py:556
  6.5 0.9 %early.1 = (f32[4224,128]{1,0:T(8,128)S(1)}, bf16[2,2,256,1024]{3,2,1,0:T(8,128)(2,1)S(1)}) custom-call(f32[4224,128]{1,0:T(8,128)S(1)} %get-tuple-element.18.conv_in, f32[8192,128]{1,0:T(8,128)S(1)} %get-tuple-element.19.held, bf16[4,2,256,1024]{3,2,1,0:T(8,128)(2,1)S(1)} %get-tuple-element.20.inputs, ...), custom_call_target="tpu_custom_call", output_to_operand_aliasing={{0}: (0, {})} | custom-call | tf_op jit(solution)/shard_map/early/pallas_call | solution.py:557
  7.4 0.0 collective-permute-done.received
  7.4 3.1 %second.1 = (bf16[256,2048]{1,0:T(8,128)(2,1)}, bf16[256,2048]{1,0:T(8,128)(2,1)}, bf16[256,2048]{1,0:T(8,128)(2,1)}, bf16[256,2048]{1,0:T(8,128)(2,1)}, f32[8,2048]{1,0:T(8,128)}) custom-call(bf16[2,2,256,1024]{3,2,1,0:T(8,128)(2,1)S(1)} %get-tuple-element.22.early, f32[18432,128]{1,0:T(8,128)S(1)} %get-tuple-element.23.ahead, ...), custom_call_target="tpu_custom_call" | custom-call | tf_op jit(solution)/shard_map/second/pallas_call | solution.py:569
Async XLA Ops:
  5.7 1.7 %collective-permute-start = (bf16[2,8,16,128]{3,2,1,0:T(8,128)(2,1)S(1)}, bf16[2,8,16,128]{3,2,1,0:T(8,128)(2,1)S(1)}, u32[]{:S(2)}, u32[]{:S(2)}) collective-permute-start(bf16[2,8,16,128]{3,2,1,0:T(8,128)(2,1)S(1)} %get-tuple-element.24.sent), channel_id=1, source_target_pairs={{0,4},{4,0},{1,5},{5,1},{2,6},{6,2},{3,7},{7,3},{8,12},{12,8},{9,1... | collective-permute-start | bytes 196616 | tf_op jit(solution)/shard_map/ppermute | solution.py:556

commit v6 on v4

--- a/solution.py
+++ b/solution.py
@@ -277,11 +277,12 @@
 ):
     direction = lax.axis_index("ctx")
     sources = (q, dy, v, k)
-    start_coefficients(rates_hbm, res_hbm, coef, coef_sem)
     for half in range(shape.halves):
         for chunk in range(shape.chunks):
             for j in range(4):
                 in_copy(shape, j, half, direction, chunk, sources[j], inputs, in_sem).start()
+            if half + chunk == 0:
+                start_coefficients(rates_hbm, res_hbm, coef, coef_sem)
     wait_all(coef, coef_sem)
     scale[...] = mode_tables(coef[0], coef[1], table)
     zeros = (jnp.zeros((GROUPS, LANES), F32),) * shape.modes

time: 10.8 us -> 10.8 us (level)
  no operation moved by 1% of the time
where the time goes in v6:
time: 10.8 us; the launch traced here: 10.6 us
  Pallas kernels  9.24 us (86%)
  starting transfers between devices  0.73 us (7%)
  between operations  0.66 us (6%)
    pallas_call x1, Pallas kernels, pair(): pl.pallas_call(functools.partial(first_kernel, shape), in_specs=[HBM] * 6...  5.2 us
    pallas_call x1, Pallas kernels, pair(): pl.pallas_call(functools.partial(second_kernel, shape), in_specs=[VMEM] *...  3.11 us
    pallas_call x1, Pallas kernels, pair(): pl.pallas_call(functools.partial(early_kernel, shape), in_specs=[VMEM] *...  0.94 us
    ppermute x1, starting transfers between devices, pair(): received = lax.ppermute(sent, 'ctx', [(0, 1), (1, 0)])  0.73 us
  transfers between devices with their start and end apart: 1, of which 0 were waited for; matrix products, arithmetic and copies ran while one was open for 0% of the time, Pallas kernels for 9%

profile of v6, /device:TPU:3, one launch (start us, length us, event | category | flops | bytes accessed | tf_op | source)
XLA Modules:
  0.0 10.6 jit_solution(18095660435478885451)
XLA Ops:
  0.6 5.2 %first.1 = (f32[4224,128]{1,0:T(8,128)S(1)}, f32[18432,128]{1,0:T(8,128)S(1)}, f32[8192,128]{1,0:T(8,128)S(1)}, bf16[4,2,256,1024]{3,2,1,0:T(8,128)(2,1)S(1)}, b...) custom-call(bf16[256,2048]{1,0:T(8,128)(2,1)} %q.1, bf16[256,2048]{1,0:T(8,128)(2,1)} %dy.1, ...), custom_call_target="tpu_custom_call" | custom-call | tf_op jit(solution)/shard_map/first/pallas_call | solution.py:506
  5.8 0.7 %collective-permute-start = (bf16[2,8,16,128]{3,2,1,0:T(8,128)(2,1)S(1)}, bf16[2,8,16,128]{3,2,1,0:T(8,128)(2,1)S(1)}, u32[]{:S(2)}, u32[]{:S(2)}) collective-permute-start(bf16[2,8,16,128]{3,2,1,0:T(8,128)(2,1)S(1)} %get-tuple-element.24.sent), channel_id=1, source_target_pairs={{0,4},{4,0},{1,5},{5,1},{2,6},{6,2},{3,7},{7,3},{8,12},{12,8},{9,1... | collective-permute-start | bytes 196616 | tf_op jit(solution)/shard_map/ppermute | solution.py:528
  6.6 0.9 %early.1 = (f32[4224,128]{1,0:T(8,128)S(1)}, bf16[2,2,256,1024]{3,2,1,0:T(8,128)(2,1)S(1)}) custom-call(f32[4224,128]{1,0:T(8,128)S(1)} %get-tuple-element.18.conv_in, f32[8192,128]{1,0:T(8,128)S(1)} %get-tuple-element.19.held, bf16[4,2,256,1024]{3,2,1,0:T(8,128)(2,1)S(1)} %get-tuple-element.20.inputs, ...), custom_call_target="tpu_custom_call", output_to_operand_aliasing={{0}: (0, {})} | custom-call | tf_op jit(solution)/shard_map/early/pallas_call | solution.py:529
  7.5 0.0 collective-permute-done.received
  7.5 3.1 %second.1 = (bf16[256,2048]{1,0:T(8,128)(2,1)}, bf16[256,2048]{1,0:T(8,128)(2,1)}, bf16[256,2048]{1,0:T(8,128)(2,1)}, bf16[256,2048]{1,0:T(8,128)(2,1)}, f32[8,2048]{1,0:T(8,128)}) custom-call(bf16[2,2,256,1024]{3,2,1,0:T(8,128)(2,1)S(1)} %get-tuple-element.22.early, f32[18432,128]{1,0:T(8,128)S(1)} %get-tuple-element.23.ahead, ...), custom_call_target="tpu_custom_call" | custom-call | tf_op jit(solution)/shard_map/second/pallas_call | solution.py:541
Async XLA Ops:
  5.8 1.7 %collective-permute-start = (bf16[2,8,16,128]{3,2,1,0:T(8,128)(2,1)S(1)}, bf16[2,8,16,128]{3,2,1,0:T(8,128)(2,1)S(1)}, u32[]{:S(2)}, u32[]{:S(2)}) collective-permute-start(bf16[2,8,16,128]{3,2,1,0:T(8,128)(2,1)S(1)} %get-tuple-element.24.sent), channel_id=1, source_target_pairs={{0,4},{4,0},{1,5},{5,1},{2,6},{6,2},{3,7},{7,3},{8,12},{12,8},{9,1... | collective-permute-start | bytes 196616 | tf_op jit(solution)/shard_map/ppermute | solution.py:528
